TPU v7x, 256 devices: a whole 4x4x8 slice. The times are simulated.
256 devices in a mesh: fsdp: 16 (over x_lo, z), expert: 16 (over y, x_hi, core).
Axes of the slice: x: 4 (x_hi: 2, x_lo: 2; x = x_hi * 2 + x_lo), y: 4, z: 8, core: 2. Of those that a mesh axis runs over, the one named last changes fastest.
Arguments:
- tokens: bfloat16 [2048, 3072], P('expert'), may hold values from -6 to 6
- cotangent: bfloat16 [2048, 3072], P('expert'), may hold values from -6 to 6
- expert_ids: int32 [2048, 4], P('expert'), may hold values from 0 to 15, all different within a row; in each aligned block of 128 rows (0 to 127, 128 to 255, ...) at most 40 rows name the same one
- gate_values: bfloat16 [2048, 4], P('expert'), may hold values from 0.049804688 to 0.5
- w_in: bfloat16 [3072, 16, 6144], P(None, 'expert', 'fsdp'), may hold values from -0.109375 to 0.109375
- w_out: bfloat16 [6144, 16, 3072], P('fsdp', 'expert'), may hold values from -0.078125 to 0.078125
Outputs:
- grad_tokens: bfloat16 [2048, 3072], P('expert')
- grad_gates: bfloat16 [2048, 4], P('expert')
- grad_w_in: bfloat16 [3072, 16, 6144], P(None, 'expert', 'fsdp')
- grad_w_out: bfloat16 [6144, 16, 3072], P('fsdp', 'expert')
Inputs may be any that keep to these rules, and one draw needn't show every extreme that they name: `expert_ids`: in each aligned block of 128 rows (the rows of one index of the expert axis) the 4 entries of a row differ, no expert is named by more than 40 rows, a bound that some block reaches.
All inputs are finite; a program needn't handle non-finite values.
Results may differ from a plain program's by a relative error of at most 0.0049.
Values may be sent and summed in bfloat16 or wider, within the bound.
A program may use at most 128 MiB of HBM per device.

v0:
```python
import jax
import jax.numpy as jnp
from jax import lax
from jax.sharding import PartitionSpec as P

EXPERTS = 16
CAP = 40


def slot_targets(expert_ids):
    flat = expert_ids.reshape(-1)
    table = (flat[:, None] == jnp.arange(EXPERTS, dtype=jnp.int32)[None, :]).astype(jnp.int32)
    earlier = jnp.cumsum(table, axis=0) - table
    position = jnp.sum(earlier * table, axis=1)
    return flat * CAP + position


def fill_slots(rows, target):
    holder = jnp.zeros((EXPERTS * CAP,) + rows.shape[1:], rows.dtype)
    return holder.at[target].set(rows)


def local(tokens, cotangent, expert_ids, gate_values, w_in, w_out):
    tok_rows, model_width = tokens.shape
    top_count = expert_ids.shape[1]
    n_source = lax.axis_size("expert")
    local_count = EXPERTS // n_source
    target = slot_targets(expert_ids)
    send_x = fill_slots(jnp.repeat(tokens, top_count, axis=0), target).reshape(
        EXPERTS, CAP, model_width
    )
    send_g = fill_slots(jnp.repeat(cotangent, top_count, axis=0), target).reshape(
        EXPERTS, CAP, model_width
    )
    send_gate = fill_slots(gate_values.reshape(-1), target).reshape(EXPERTS, CAP)
    arrived_x, arrived_g, arrived_gate = (
        lax.all_to_all(send_x, "expert", split_axis=0, concat_axis=0, tiled=True),
        lax.all_to_all(send_g, "expert", split_axis=0, concat_axis=0, tiled=True),
        lax.all_to_all(send_gate, "expert", split_axis=0, concat_axis=0, tiled=True),
    )
    slot_x = arrived_x.reshape(n_source, local_count, CAP, model_width)
    slot_g = arrived_g.reshape(n_source, local_count, CAP, model_width)
    gate_four = arrived_gate.reshape(n_source, local_count, CAP, 1).astype(jnp.float32)
    pre_act = jnp.einsum("blcd,dlf->blcf", slot_x, w_in, preferred_element_type=jnp.float32)
    upstream = jnp.einsum("blcd,fld->blcf", slot_g, w_out, preferred_element_type=jnp.float32)
    squash = jax.nn.sigmoid(pre_act)
    active = pre_act * squash
    gate_part = jnp.sum(active * upstream, axis=-1)
    act_gated = (gate_four * active).astype(jnp.bfloat16)
    grad_pre = (gate_four * squash * (1.0 + pre_act * (1.0 - squash)) * upstream).astype(
        jnp.bfloat16
    )
    part_x = jnp.einsum("blcf,dlf->blcd", grad_pre, w_in, preferred_element_type=jnp.float32)
    grad_in = jnp.einsum(
        "blcd,blcf->dlf", slot_x, grad_pre, preferred_element_type=jnp.float32
    ).astype(jnp.bfloat16)
    grad_out = jnp.einsum(
        "blcf,blcd->fld", act_gated, slot_g, preferred_element_type=jnp.float32
    ).astype(jnp.bfloat16)
    sum_x, sum_gate = lax.psum((part_x, gate_part), "fsdp")
    back_x, back_gate = (
        lax.all_to_all(
            sum_x.reshape(EXPERTS, CAP, model_width),
            "expert",
            split_axis=0,
            concat_axis=0,
            tiled=True,
        ),
        lax.all_to_all(
            sum_gate.reshape(EXPERTS, CAP), "expert", split_axis=0, concat_axis=0, tiled=True
        ),
    )
    picked = back_x.reshape(EXPERTS * CAP, model_width)[target]
    grad_tokens = picked.reshape(tok_rows, top_count, model_width).sum(axis=1).astype(jnp.bfloat16)
    grad_gates = (
        back_gate.reshape(EXPERTS * CAP)[target].reshape(tok_rows, top_count).astype(jnp.bfloat16)
    )
    return (grad_tokens, grad_gates, grad_in, grad_out)


def solution(mesh):
    return jax.shard_map(
        local,
        mesh=mesh,
        in_specs=(
            P("expert", None),
            P("expert", None),
            P("expert", None),
            P("expert", None),
            P(None, "expert", "fsdp"),
            P("fsdp", "expert", None),
        ),
        out_specs=(
            P("expert", None),
            P("expert", None),
            P(None, "expert", "fsdp"),
            P("fsdp", "expert", None),
        ),
        check_vma=False,
    )
```

profile of v0, /device:TPU:1, one launch (start us, length us, event | category | flops | bytes accessed | tf_op | source)
XLA Modules:
  0.0 484.1 jit_solution(4626773930175029390)
XLA Ops:
  7.2 0.0 copy-start
  7.2 0.8 broadcast_multiply_fusion
  8.0 0.8 copy.29
  8.8 0.1 eq.29
  8.9 0.1 eq.25
  9.0 0.8 copy.32
  9.8 0.1 reshape.170
  10.0 0.1 copy.28
  10.1 0.1 mul.50
  10.2 1.2 reduce-window.6
  11.3 0.2 slice_reduce_fusion
  11.6 0.1 fusion.27
  11.7 3.8 scatter_custom_fusion
  15.5 0.7 all_to_all.25
  16.2 8.4 %all-to-all-start = ((bf16[16,1,40]{2,1,0:T(2,128)(2,1)}), bf16[16,1,40]{2,1,0:T(2,128)(2,1)S(1)}, u32[]{:S(2)}, u32[]{:S(2)}) async-start(bf16[16,1,40]{2,1,0:T(2,128)(2,1)} %all_to_all.25), calls=%async_computation | async-start | bytes 16384 | tf_op jit(solution)/shard_map/all_to_all | solution.py:39
  24.6 3.7 broadcast_in_dim.7
  28.4 5.9 %reshape.178 = bf16[512,3072]{1,0:T(8,128)(2,1)} reshape(bf16[128,4,3072]{2,1,0:T(4,128)(2,1)} %broadcast_in_dim.7) | data formatting | bytes 6291456 | tf_op jit(solution)/shard_map/reshape | solution.py:29
  34.3 8.8 %scatter_custom_fusion.1 = bf16[640,3072]{1,0:T(8,128)(2,1)} fusion(s32[512]{0:T(512)S(1)} %bitcast.88, bf16[512,3072]{1,0:T(8,128)(2,1)} %reshape.178, bf16[]{:T(256)} %constant.6.clone.1), kind=kCustom, calls=%fused_computation.17 | custom fusion | bytes 3932672 | tf_op jit(solution)/shard_map/scatter | solution.py:20
  43.2 7.4 %all-to-all-start.1 = ((bf16[16,40,3072]{2,1,0:T(8,128)(2,1)}), bf16[16,40,3072]{2,1,0:T(8,128)(2,1)}, u32[]{:S(2)}, u32[]{:S(2)}) async-start(bf16[16,40,3072]{2,1,0:T(8,128)(2,1)} %bitcast.85), calls=%async_computation.1 | async-start | bytes 7864320 | tf_op jit(solution)/shard_map/all_to_all | solution.py:37
  50.5 2.6 broadcast_in_dim.8
  53.2 5.9 %reshape.186 = bf16[512,3072]{1,0:T(8,128)(2,1)} reshape(bf16[128,4,3072]{2,1,0:T(4,128)(2,1)} %broadcast_in_dim.8) | data formatting | bytes 6291456 | tf_op jit(solution)/shard_map/reshape | solution.py:32
  59.1 8.6 %scatter_custom_fusion.2 = bf16[640,3072]{1,0:T(8,128)(2,1)} fusion(s32[512]{0:T(512)S(1)} %bitcast.89, bf16[512,3072]{1,0:T(8,128)(2,1)} %reshape.186, bf16[]{:T(256)} %constant.6.clone.1), kind=kCustom, calls=%fused_computation.15 | custom fusion | bytes 3932672 | tf_op jit(solution)/shard_map/scatter | solution.py:20
  67.7 30.9 %all-to-all-done.1 = bf16[16,40,3072]{2,1,0:T(8,128)(2,1)} async-done(((bf16[16,40,3072]{2,1,0:T(8,128)(2,1)}), bf16[16,40,3072]{2,1,0:T(8,128)(2,1)}, u32[]{:S(2)}, u32[]{:S(2)}) %all-to-all-start.1) | async-done | bytes 3932192 | tf_op jit(solution)/shard_map/all_to_all | solution.py:37
  98.6 5.3 %all-to-all-start.2 = ((bf16[16,40,3072]{2,1,0:T(8,128)(2,1)}), bf16[16,40,3072]{2,1,0:T(8,128)(2,1)}, u32[]{:S(2)}, u32[]{:S(2)}) async-start(bf16[16,40,3072]{2,1,0:T(8,128)(2,1)} %bitcast.86), calls=%async_computation.2 | async-start | bytes 7864320 | tf_op jit(solution)/shard_map/all_to_all | solution.py:38
  103.9 0.6 all-reduce.2.cloned.1.call-start
  104.5 5.3 %fusion.12 = f32[16,1,40,384]{3,2,0,1:T(8,128)} fusion(bf16[16,40,3072]{2,1,0:T(8,128)(2,1)} %all-to-all-done.1, bf16[3072,1,384]{2,0,1:T(8,128)(2,1)S(1)} %copy-done), kind=kOutput, calls=%fused_computation.19 | convolution fusion | flops 1509949440 | bytes 7274496 | tf_op jit(solution)/shard_map/blcd,dlf->blcf/dot_general | solution.py:44
  109.9 42.3 %all-to-all-done.2 = bf16[16,40,3072]{2,1,0:T(8,128)(2,1)} async-done(((bf16[16,40,3072]{2,1,0:T(8,128)(2,1)}), bf16[16,40,3072]{2,1,0:T(8,128)(2,1)}, u32[]{:S(2)}, u32[]{:S(2)}) %all-to-all-start.2) | async-done | bytes 3932192 | tf_op jit(solution)/shard_map/all_to_all | solution.py:38
  152.1 5.5 %multiply_reduce_fusion = (f32[16,40]{1,0:T(8,128)S(1)}, bf16[16,1,40,384]{3,2,0,1:T(8,128)(2,1)S(1)}) fusion(f32[16,1,40,384]{3,2,0,1:T(8,128)} %fusion.12, f32[16,40]{1,0:T(8,128)S(1)} %bitcast.92, bf16[16,40,3072]{2,1,0:T(8,128)(2,1)} %all-to-all-done.2, bf16[384,1,3072]{2,0,1:T(8,128)(2,1)} %param.11), kind=kOutput, calls=%fused_computation.22 | convolution fusion | flops 1513143680 | bytes 7771136 | tf_op jit(solution)/shard_map/blcd,fld->blcf/dot_general | solution.py:45
  157.7 5.3 %fusion.4 = f32[16,40,3072]{2,1,0:T(8,128)} fusion(bf16[3072,1,384]{2,0,1:T(8,128)(2,1)S(1)} %copy-done, bf16[16,1,40,384]{3,2,0,1:T(8,128)(2,1)S(1)} %get-tuple-element.21), kind=kOutput, calls=%fused_computation.11 | convolution fusion | flops 1509949440 | bytes 10715136 | tf_op jit(solution)/shard_map/blcf,dlf->blcd/dot_general | solution.py:53
  163.0 0.0 all-reduce.2.cloned.1.call-update
  163.0 33.6 %psum.15 = f32[16,1,40]{2,1,0:T(1,128)S(1)} all-reduce(f32[16,1,40]{2,1,0:T(1,128)S(1)} %bitcast.94), channel_id=1, replica_groups=mesh['fsdp'=16,'expert'=16] {'fsdp'}, use_global_device_ids=true, to_apply=%region_9.10 | all-reduce | flops 640 | bytes 5120 | tf_op jit(solution)/shard_map/psum | solution.py:60
  196.6 16.6 %all_to_all.31 = f32[16,1,40]{2,1,0:T(1,128)S(1)} all-to-all(f32[16,1,40]{2,1,0:T(1,128)S(1)} %psum.15), channel_id=1, replica_groups=mesh['fsdp'=16,'expert'=16] {'expert'}, dimensions={0} | all-to-all | bytes 5120 | tf_op jit(solution)/shard_map/all_to_all | solution.py:69
  213.2 140.1 %all-reduce.2.cloned.1.call-done = f32[16,40,3072]{2,1,0:T(8,128)} async-done(((f32[16,40,3072]{2,1,0:T(8,128)}), f32[16,40,3072]{2,1,0:T(8,128)}) %all-reduce.2.cloned.1.call-update) | async-done | bytes 7864336 | tf_op jit(solution)/shard_map/psum | solution.py:60
  353.2 7.6 %all-to-all-start.3 = ((f32[16,40,3072]{2,1,0:T(8,128)}), f32[16,40,3072]{2,1,0:T(8,128)}, u32[]{:S(2)}, u32[]{:S(2)}) async-start(f32[16,40,3072]{2,1,0:T(8,128)} %all-reduce.2.cloned.1.call-done), calls=%async_computation.3 | async-start | bytes 15728640 | tf_op jit(solution)/shard_map/all_to_all | solution.py:62
  360.8 4.1 fusion
  365.0 2.4 copy.35
  367.4 4.9 %fusion.1 = bf16[384,1,3072]{0,2,1:T(8,128)(2,1)S(1)} fusion(bf16[16,40,3072]{2,1,0:T(8,128)(2,1)} %all-to-all-done.2, f32[16,40]{1,0:T(8,128)S(1)} %bitcast.93, f32[16,1,40,384]{3,2,0,1:T(8,128)} %fusion.12), kind=kOutput, calls=%fused_computation.8 | convolution fusion | flops 1512603648 | bytes 7277056 | tf_op jit(solution)/shard_map/blcf,blcd->fld/dot_general | solution.py:57
  372.4 2.6 copy.36
  375.0 0.5 broadcast.81
  375.5 0.7 reduce.6
  376.1 0.1 reshape.147
  376.2 3.5 gather_fusion.1
  379.8 0.1 convert_element_type.58
  379.9 0.7 copy.34
  380.5 70.4 %all-to-all-done.3 = f32[16,40,3072]{2,1,0:T(8,128)} async-done(((f32[16,40,3072]{2,1,0:T(8,128)}), f32[16,40,3072]{2,1,0:T(8,128)}, u32[]{:S(2)}, u32[]{:S(2)}) %all-to-all-start.3) | async-done | bytes 7864352 | tf_op jit(solution)/shard_map/all_to_all | solution.py:62
  450.9 10.6 %gather_fusion = f32[512,3072]{1,0:T(8,128)} fusion(f32[640,3072]{1,0:T(8,128)} %bitcast.19, s32[1024]{0:T(1024)S(1)} %pad_clamp_fusion), kind=kCustom, calls=%fused_computation | custom fusion | bytes 12584960 | tf_op jit(solution)/shard_map/gather | solution.py:73
  461.5 7.9 %reshape.146 = f32[128,4,3072]{2,1,0:T(4,128)} reshape(f32[512,3072]{1,0:T(8,128)} %gather_fusion) | data formatting | bytes 12582912 | tf_op jit(solution)/shard_map/reshape | solution.py:74
  469.5 7.5 %reduce_sum.33 = bf16[128,3072]{1,0:T(8,128)(2,1)} reduce(f32[128,4,3072]{2,1,0:T(4,128)} %reshape.146, f32[]{:T(128)} %constant.5.clone.1), dimensions={1}, to_apply=%region_7.8 | reduce | flops 1179648 | bytes 7077892 | tf_op jit(solution)/shard_map/reduce_sum | solution.py:74
  (12 shorter events, 0.1 us)
Async XLA Ops:
  7.2 97.4 %copy-start = (bf16[3072,1,384]{2,0,1:T(8,128)(2,1)S(1)}, bf16[3072,1,384]{2,0,1:T(8,128)(2,1)}, u32[]{:S(2)}) copy-start(bf16[3072,1,384]{2,0,1:T(8,128)(2,1)} %param.10) | copy-start | bytes 7077892
  16.2 27.0 %all-to-all-start = ((bf16[16,1,40]{2,1,0:T(2,128)(2,1)}), bf16[16,1,40]{2,1,0:T(2,128)(2,1)S(1)}, u32[]{:S(2)}, u32[]{:S(2)}) async-start(bf16[16,1,40]{2,1,0:T(2,128)(2,1)} %all_to_all.25), calls=%async_computation | async-start | bytes 16384 | tf_op jit(solution)/shard_map/all_to_all | solution.py:39
  43.2 7.4 %copy-start.2 = (bf16[128,3072]{1,0:T(8,128)(2,1)S(1)}, bf16[128,3072]{1,0:T(8,128)(2,1)}, u32[]{:S(2)}) copy-start(bf16[128,3072]{1,0:T(8,128)(2,1)} %param.7) | copy-start | bytes 2359300
  43.2 55.5 %all-to-all-start.1 = ((bf16[16,40,3072]{2,1,0:T(8,128)(2,1)}), bf16[16,40,3072]{2,1,0:T(8,128)(2,1)}, u32[]{:S(2)}, u32[]{:S(2)}) async-start(bf16[16,40,3072]{2,1,0:T(8,128)(2,1)} %bitcast.85), calls=%async_computation.1 | async-start | bytes 7864320 | tf_op jit(solution)/shard_map/all_to_all | solution.py:37
  98.6 53.5 %all-to-all-start.2 = ((bf16[16,40,3072]{2,1,0:T(8,128)(2,1)}), bf16[16,40,3072]{2,1,0:T(8,128)(2,1)}, u32[]{:S(2)}, u32[]{:S(2)}) async-start(bf16[16,40,3072]{2,1,0:T(8,128)(2,1)} %bitcast.86), calls=%async_computation.2 | async-start | bytes 7864320 | tf_op jit(solution)/shard_map/all_to_all | solution.py:38
  103.9 249.3 %all-reduce.2.cloned.1.call-start = ((), (), s32[]{:S(2)}) async-start(), calls=%async_computation.5 | async-start | bytes 15728640 | tf_op jit(solution)/shard_map/psum | solution.py:60
  353.2 97.7 %all-to-all-start.3 = ((f32[16,40,3072]{2,1,0:T(8,128)}), f32[16,40,3072]{2,1,0:T(8,128)}, u32[]{:S(2)}, u32[]{:S(2)}) async-start(f32[16,40,3072]{2,1,0:T(8,128)} %all-reduce.2.cloned.1.call-done), calls=%async_computation.3 | async-start | bytes 15728640 | tf_op jit(solution)/shard_map/all_to_all | solution.py:62
  461.5 15.5 %copy-start.1 = (bf16[3072,1,384]{2,0,1:T(8,128)(2,1)S(1)}, bf16[3072,1,384]{2,0,1:T(8,128)(2,1)}, u32[]{:S(2)}) copy-start(bf16[3072,1,384]{2,0,1:T(8,128)(2,1)} %param.10) | copy-start | bytes 7077892
Sparse Core Ops, SparseCore 0:
  163.2 190.0 all-reduce.1
where the time goes:
time: 493 us; the launch traced here: 484 us
  waiting for transfers between devices  284 us (58%)
  local copies, waits for them, and re-layouts  71 us (14%)
  blocking collectives  50.1 us (10%)
  starting transfers between devices  29.2 us (6%)
  matrix products  25.2 us (5%)
  between operations  14.4 us (3%)
  other arithmetic  10.3 us (2%)
    psum x1, waiting for transfers between devices, local(): sum_x, sum_gate = lax.psum((part_x, gate_part), 'fsdp')  140 us
    all_to_all x1, waiting for transfers between devices, local(): lax.all_to_all(sum_x.reshape(EXPERTS, CAP, model_width), 'expert', split_...  70.4 us
    all_to_all x1, waiting for transfers between devices, local(): lax.all_to_all(send_g, 'expert', split_axis=0, concat_axis=0, tiled=True)  42.3 us
    psum x1, blocking collectives, local(): sum_x, sum_gate = lax.psum((part_x, gate_part), 'fsdp')  33.6 us
    all_to_all x1, waiting for transfers between devices, local(): lax.all_to_all(send_x, 'expert', split_axis=0, concat_axis=0, tiled=True)  30.9 us
    scatter x3, local copies, waits for them, and re-layouts, fill_slots(): return holder.at[target].set(rows)  21.2 us
    all_to_all x1, blocking collectives, local(): lax.all_to_all(sum_gate.reshape(EXPERTS, CAP), 'expert', split_axis=0, co...  16.6 us
    gather x1, local copies, waits for them, and re-layouts, local(): picked = back_x.reshape(EXPERTS * CAP, model_width)[target]  10.6 us
  transfers between devices with their start and end apart: 5, of which 4 were waited for; matrix products, arithmetic and copies ran while one was open for 13% of the time, Pallas kernels for 0%

commit v1 on v0

v1 whole, which is shorter than its diff:
```python
import jax
import jax.numpy as jnp
from jax import lax
from jax.sharding import PartitionSpec as P

EXPERTS = 16
CAP = 40
F32 = jnp.float32
BF16 = jnp.bfloat16


def local(tokens, cotangent, expert_ids, gate_values, w_in, w_out):
    rows, width = tokens.shape
    n_f = lax.axis_size("fsdp")
    part = 2 * width // n_f
    me_f = lax.axis_index("fsdp")
    half = me_f // (n_f // 2)
    col = (me_f % (n_f // 2)) * part

    ids_t = expert_ids.T
    experts = jnp.arange(EXPERTS, dtype=jnp.int32)[:, None]
    hit = ids_t[None] == experts[:, :, None]
    named = jnp.any(hit, axis=1)
    gates_of = jnp.sum(jnp.where(hit, gate_values.T[None].astype(F32), 0.0), axis=1)
    before = jnp.arange(rows)[:, None] < jnp.arange(rows)[None, :]
    place = jnp.dot(
        named.astype(BF16), before.astype(BF16), preferred_element_type=F32
    ).astype(jnp.int32)
    slots = jnp.arange(CAP, dtype=jnp.int32)[None, :, None]
    pick = ((place[:, None, :] == slots) & named[:, None, :]).reshape(EXPERTS * CAP, rows)
    pick_b = pick.astype(BF16)
    gate_send = jnp.sum(
        jnp.where(pick.reshape(EXPERTS, CAP, rows), gates_of[:, None, :], 0.0), axis=2
    )

    chosen = jnp.where(half == 0, lax.dynamic_slice_in_dim(tokens, col, part, 1),
                       lax.dynamic_slice_in_dim(cotangent, col, part, 1))
    send = jnp.dot(pick_b, chosen, preferred_element_type=F32).astype(BF16)
    send = send.reshape(EXPERTS, CAP, part)
    got = lax.all_to_all(send, "expert", split_axis=0, concat_axis=0, tiled=True)
    gate_got = lax.all_to_all(gate_send, "expert", split_axis=0, concat_axis=0, tiled=True)
    every = lax.all_gather(got.reshape(EXPERTS * CAP, part), "fsdp", axis=0)
    xs, gs = every[: n_f // 2], every[n_f // 2 :]
    win = w_in.reshape(n_f // 2, part, -1)
    wout = w_out.reshape(-1, n_f // 2, part)
    pre = jnp.einsum("zsd,zdf->sf", xs, win, preferred_element_type=F32)
    up = jnp.einsum("zsd,fzd->sf", gs, wout, preferred_element_type=F32)
    gate = gate_got.reshape(EXPERTS * CAP, 1)
    squash = jax.nn.sigmoid(pre)
    active = pre * squash
    gate_part = jnp.sum(active * up, axis=-1)
    act_gated = (gate * active).astype(BF16)
    grad_pre = (gate * squash * (1.0 + pre * (1.0 - squash)) * up).astype(BF16)
    w16 = w_in.reshape(n_f, width // n_f, -1)
    part_x = jnp.einsum("sf,zdf->zsd", grad_pre, w16, preferred_element_type=F32)
    mine = lax.psum_scatter(part_x, "fsdp", scatter_dimension=0, tiled=False)
    gate_sum = lax.psum(gate_part.reshape(EXPERTS, CAP), "fsdp")
    back_x = lax.all_to_all(mine.reshape(EXPERTS, CAP, -1), "expert", 0, 0, tiled=True)
    back_gate = lax.all_to_all(gate_sum, "expert", split_axis=0, concat_axis=0, tiled=True)
    grad_in = jnp.einsum("zsd,sf->zdf", xs, grad_pre, preferred_element_type=F32).astype(BF16)
    grad_out = jnp.einsum("sf,zsd->fzd", act_gated, gs, preferred_element_type=F32).astype(BF16)
    tok = jnp.dot(
        pick.astype(F32).T, back_x.reshape(EXPERTS * CAP, -1),
        precision=lax.Precision.HIGHEST, preferred_element_type=F32,
    ).astype(BF16)
    grad_tokens = lax.all_gather(tok, "fsdp", axis=1, tiled=True)
    by_expert = jnp.sum(
        jnp.where(pick.reshape(EXPERTS, CAP, rows), back_gate[:, :, None], 0.0), axis=1
    )
    grad_gates = jnp.sum(jnp.where(hit, by_expert[:, None, :], 0.0), axis=0).T.astype(BF16)
    return (
        grad_tokens,
        grad_gates,
        grad_in.reshape(w_in.shape),
        grad_out.reshape(w_out.shape),
    )


def solution(mesh):
    return jax.shard_map(
        local,
        mesh=mesh,
        in_specs=(
            P("expert", None),
            P("expert", None),
            P("expert", None),
            P("expert", None),
            P(None, "expert", "fsdp"),
            P("fsdp", "expert", None),
        ),
        out_specs=(
            P("expert", None),
            P("expert", None),
            P(None, "expert", "fsdp"),
            P("fsdp", "expert", None),
        ),
        check_vma=False,
    )
```

time: 493 us -> 351 us (0.71)
  the two profiles are of different devices: /device:TPU:1 before, /device:TPU:6 now
where the time goes in v1:
time: 351 us; the launch traced here: 349 us
  waiting for transfers between devices  181 us (52%)
  blocking collectives  96.2 us (27%)
  matrix products  26.2 us (7%)
  starting transfers between devices  14.6 us (4%)
  between operations  14.2 us (4%)
  local copies, waits for them, and re-layouts  12.7 us (4%)
  other arithmetic  4.41 us (1%)
    all_gather x1, waiting for transfers between devices, local(): every = lax.all_gather(got.reshape(EXPERTS * CAP, part), 'fsdp', axis=0)  92 us
    reduce_scatter x1, waiting for transfers between devices, local(): mine = lax.psum_scatter(part_x, 'fsdp', scatter_dimension=0, tiled=False)  78.9 us
    all_gather x1, blocking collectives, local(): grad_tokens = lax.all_gather(tok, 'fsdp', axis=1, tiled=True)  35.9 us
    psum x1, blocking collectives, local(): gate_sum = lax.psum(gate_part.reshape(EXPERTS, CAP), 'fsdp')  33.5 us
    all_to_all x1, blocking collectives, local(): lax.all_to_all(send, 'expert', split_axis=0, concat_axis=0, tiled=True)  16.7 us
    all_to_all x1, blocking collectives, local(): lax.all_to_all(gate_send, 'expert', split_axis=0, concat_axis=0, tiled=True)  10.1 us
    unnamed x15, local copies, waits for them, and re-layouts  9.86 us
    all_to_all x1, starting transfers between devices, local(): lax.all_to_all(mine.reshape(EXPERTS, CAP, -1), 'expert', 0, 0, tiled=True)  7.28 us
  transfers between devices with their start and end apart: 4, of which 4 were waited for; matrix products, arithmetic and copies ran while one was open for 6% of the time, Pallas kernels for 0%

profile of v1, /device:TPU:6, one launch (start us, length us, event | category | flops | bytes accessed | tf_op | source)
XLA Modules:
  0.0 348.9 jit_solution(9001200368042260039)
XLA Ops:
  7.2 0.0 copy-start
  7.2 0.0 copy-start.4
  7.2 0.0 all-gather.2.cloned.1.call-start
  7.3 0.8 fusion.27
  8.1 0.1 convolution_convert_fusion.2
  8.2 0.1 eq.50
  8.3 0.2 fusion.19
  8.5 1.2 convolution_convert_fusion.1
  9.7 16.7 %all_to_all.28 = bf16[16,40,384]{2,1,0:T(8,128)(2,1)} all-to-all(bf16[16,40,384]{2,1,0:T(8,128)(2,1)S(1)} %bitcast.59), channel_id=1, replica_groups=mesh['fsdp'=16,'expert'=16] {'expert'}, dimensions={0} | all-to-all | bytes 983040 | tf_op jit(solution)/shard_map/all_to_all | solution.py:40
  26.4 0.0 all-gather.2.cloned.1.call-update
  26.5 3.6 %copy.59 = bf16[48,8,8,384]{3,2,1,0:T(8,128)(2,1)} copy(bf16[48,8,8,384]{3,1,2,0:T(8,128)(2,1)} %bitcast.55) | data formatting | bytes 4718592
  30.1 0.0 copy-done.4
  30.1 92.0 %all-gather.2.cloned.1.call-done = bf16[16,640,384]{2,1,0:T(8,128)(2,1)} async-done(((bf16[1,640,384]{2,1,0:T(8,128)(2,1)}), bf16[16,640,384]{2,1,0:T(8,128)(2,1)}) %all-gather.2.cloned.1.call-update) | async-done | bytes 7864336 | tf_op jit(solution)/shard_map/all_gather | solution.py:42
  122.1 0.0 copy-done
  122.1 0.0 copy-start.1
  122.1 0.0 copy-start.5
  122.1 4.3 %convolution_bitcast_fusion.1 = f32[640,384]{0,1:T(8,128)S(1)} fusion(bf16[16,640,384]{2,1,0:T(8,128)(2,1)} %all-gather.2.cloned.1.call-done, bf16[8,384,384]{2,1,0:T(8,128)(2,1)S(1)} %bitcast.53), kind=kOutput, calls=%fused_computation.8 | convolution fusion | flops 1509949440 | bytes 11206656 | tf_op jit(solution)/shard_map/zsd,zdf->sf/dot_general | solution.py:46
  126.4 0.0 copy-start.2
  126.4 0.0 copy-done.1
  126.4 0.8 copy-done.5
  127.2 0.0 copy-start.3
  127.2 3.0 multiply_reduce_fusion
  130.2 0.0 copy-done.2
  130.2 0.1 all_to_all.22
  130.3 33.5 %psum.7 = f32[16,1,40]{2,1,0:T(1,128)} all-reduce(f32[16,1,40]{2,1,0:T(1,128)S(1)} %all_to_all.22), channel_id=1, replica_groups=mesh['fsdp'=16,'expert'=16] {'fsdp'}, use_global_device_ids=true, to_apply=%region_5.6 | all-reduce | flops 640 | bytes 5120 | tf_op jit(solution)/shard_map/psum | solution.py:57
  163.7 7.3 %all-to-all-start.3 = ((f32[16,1,40]{2,1,0:T(1,128)}), f32[16,1,40]{2,1,0:T(1,128)S(1)}, u32[]{:S(2)}, u32[]{:S(2)}) async-start(f32[16,1,40]{2,1,0:T(1,128)} %psum.7), calls=%async_computation.4 | async-start | bytes 16384 | tf_op jit(solution)/shard_map/all_to_all | solution.py:59
  171.0 0.0 reduce-scatter.2.cloned.1.call-start
  171.1 0.0 copy-done.3
  171.1 4.6 %all-to-all-done.3 = f32[16,1,40]{2,1,0:T(1,128)S(1)} async-done(((f32[16,1,40]{2,1,0:T(1,128)}), f32[16,1,40]{2,1,0:T(1,128)S(1)}, u32[]{:S(2)}, u32[]{:S(2)}) %all-to-all-start.3) | async-done | bytes 2592 | tf_op jit(solution)/shard_map/all_to_all | solution.py:59
  175.7 0.3 select_reduce_fusion
  176.0 10.1 %all_to_all.29 = f32[16,1,40]{2,1,0:T(1,128)S(1)} all-to-all(f32[16,1,40]{2,1,0:T(1,128)S(1)} %bitcast.61), channel_id=1, replica_groups=mesh['fsdp'=16,'expert'=16] {'expert'}, dimensions={0} | all-to-all | bytes 5120 | tf_op jit(solution)/shard_map/all_to_all | solution.py:41
  186.1 0.5 broadcast.26
  186.6 0.7 reduce.3
  187.3 0.1 mul.34
  187.4 1.9 multiply_convert_fusion.1
  189.2 4.6 %convolution_bitcast_fusion = f32[16,640,192]{1,2,0:T(8,128)} fusion(bf16[16,192,384]{2,1,0:T(8,128)(2,1)S(1)} %bitcast.52, bf16[640,384]{0,1:T(8,128)(2,1)S(1)} %multiply_convert_fusion.1), kind=kOutput, calls=%fused_computation.2 | convolution fusion | flops 1509949440 | bytes 10715136 | tf_op jit(solution)/shard_map/sf,zdf->zsd/dot_general | solution.py:55
  193.8 0.0 reduce-scatter.2.cloned.1.call-update
  193.8 0.6 select_reduce_fusion.2
  194.4 6.3 %fusion.4 = bf16[384,8,384]{0,2,1:T(8,128)(2,1)} fusion(bf16[16,640,384]{2,1,0:T(8,128)(2,1)} %all-gather.2.cloned.1.call-done, f32[640]{0:T(1024)S(1)} %mul.34, f32[640,384]{0,1:T(8,128)} %copy-done.2), kind=kOutput, calls=%fused_computation.5 | convolution fusion | flops 1512603648 | bytes 7277056 | tf_op jit(solution)/shard_map/sf,zsd->fzd/dot_general | solution.py:61
  200.7 4.3 %copy.49 = bf16[384,1,3072]{2,0,1:T(8,128)(2,1)} copy(bf16[384,1,3072]{0,2,1:T(8,128)(2,1)} %bitcast.57) | data formatting | bytes 4718592
  205.0 78.9 %reduce-scatter.2.cloned.1.call-done = f32[1,640,192]{1,2,0:T(8,128)} async-done(((f32[16,640,192]{1,2,0:T(8,128)}), f32[1,640,192]{1,2,0:T(8,128)}) %reduce-scatter.2.cloned.1.call-update) | async-done | bytes 491536 | tf_op jit(solution)/shard_map/reduce_scatter | solution.py:56
  283.8 2.1 copy.43
  285.9 7.3 %all-to-all-start.2 = ((f32[16,40,192]{2,1,0:T(8,128)}), f32[16,40,192]{2,1,0:T(8,128)S(1)}, u32[]{:S(2)}, u32[]{:S(2)}) async-start(f32[16,40,192]{2,1,0:T(8,128)} %bitcast.54), calls=%async_computation.3 | async-start | bytes 1310720 | tf_op jit(solution)/shard_map/all_to_all | solution.py:58
  293.2 6.0 %convolution_convert_fusion = bf16[8,384,384]{2,1,0:T(8,128)(2,1)} fusion(bf16[16,640,384]{2,1,0:T(8,128)(2,1)} %all-gather.2.cloned.1.call-done, bf16[640,384]{0,1:T(8,128)(2,1)S(1)} %multiply_convert_fusion.1), kind=kOutput, calls=%fused_computation.6 | convolution fusion | flops 1511129088 | bytes 10715136 | tf_op jit(solution)/shard_map/zsd,sf->zdf/dot_general | solution.py:60
  299.2 5.1 %all-to-all-done.2 = f32[16,40,192]{2,1,0:T(8,128)S(1)} async-done(((f32[16,40,192]{2,1,0:T(8,128)}), f32[16,40,192]{2,1,0:T(8,128)S(1)}, u32[]{:S(2)}, u32[]{:S(2)}) %all-to-all-start.2) | async-done | bytes 491552 | tf_op jit(solution)/shard_map/all_to_all | solution.py:58
  304.3 0.7 fusion.10
  305.0 35.9 %all_gather.7 = bf16[128,3072]{0,1:T(8,128)(2,1)S(1)} all-gather(bf16[128,192]{0,1:T(8,128)(2,1)S(1)} %fusion.10), channel_id=1, replica_groups=mesh['fsdp'=16,'expert'=16] {'fsdp'}, dimensions={1}, use_global_device_ids=true | all-gather | bytes 835584 | tf_op jit(solution)/shard_map/all_gather | solution.py:66
  340.9 1.2 copy.48
  (3 shorter events, 0.0 us)
Async XLA Ops:
  7.2 114.9 %copy-start = (bf16[3072,1,384]{2,0,1:T(8,128)(2,1)S(1)}, bf16[3072,1,384]{2,0,1:T(8,128)(2,1)}, u32[]{:S(2)}) copy-start(bf16[3072,1,384]{2,0,1:T(8,128)(2,1)} %param.10) | copy-start | bytes 7077892
  7.2 22.9 %copy-start.4 = (bf16[128,4]{0,1:T(4,128)(2,1)S(1)}, bf16[128,4]{0,1:T(4,128)(2,1)}, u32[]{:S(2)}) copy-start(bf16[128,4]{0,1:T(4,128)(2,1)} %param.9) | copy-start | bytes 3076
  7.2 114.9 %all-gather.2.cloned.1.call-start = ((), (), s32[]{:S(2)}) async-start(), calls=%async_computation.5 | async-start | bytes 8355840 | tf_op jit(solution)/shard_map/all_gather | solution.py:42
  122.1 4.3 %copy-start.1 = (bf16[48,8,8,384]{3,2,1,0:T(8,128)(2,1)S(1)}, bf16[48,8,8,384]{3,2,1,0:T(8,128)(2,1)}, u32[]{:S(2)}) copy-start(bf16[48,8,8,384]{3,2,1,0:T(8,128)(2,1)} %copy.59) | copy-start | bytes 7077892
  122.1 5.1 %copy-start.5 = (bf16[16,640,384]{2,1,0:T(8,128)(2,1)S(1)}, bf16[16,640,384]{2,1,0:T(8,128)(2,1)}, u32[]{:S(2)}) copy-start(bf16[16,640,384]{2,1,0:T(8,128)(2,1)} %all-gather.2.cloned.1.call-done) | copy-start | bytes 23592964
  126.4 3.8 %copy-start.2 = (f32[640,384]{0,1:T(8,128)}, f32[640,384]{0,1:T(8,128)S(1)}, u32[]{:S(2)}) copy-start(f32[640,384]{0,1:T(8,128)S(1)} %convolution_bitcast_fusion.1) | copy-start | bytes 2949124
  127.2 43.9 %copy-start.3 = (s32[128,4]{0,1:T(4,128)S(1)}, s32[128,4]{0,1:T(4,128)}, u32[]{:S(2)}) copy-start(s32[128,4]{0,1:T(4,128)} %param.8) | copy-start | bytes 6148
  163.7 11.9 %all-to-all-start.3 = ((f32[16,1,40]{2,1,0:T(1,128)}), f32[16,1,40]{2,1,0:T(1,128)S(1)}, u32[]{:S(2)}, u32[]{:S(2)}) async-start(f32[16,1,40]{2,1,0:T(1,128)} %psum.7), calls=%async_computation.4 | async-start | bytes 16384 | tf_op jit(solution)/shard_map/all_to_all | solution.py:59
  171.0 112.8 %reduce-scatter.2.cloned.1.call-start = ((), (), s32[]{:S(2)}) async-start(), calls=%async_computation.6 | async-start | bytes 8355840 | tf_op jit(solution)/shard_map/reduce_scatter | solution.py:56
  285.9 18.4 %all-to-all-start.2 = ((f32[16,40,192]{2,1,0:T(8,128)}), f32[16,40,192]{2,1,0:T(8,128)S(1)}, u32[]{:S(2)}, u32[]{:S(2)}) async-start(f32[16,40,192]{2,1,0:T(8,128)} %bitcast.54), calls=%async_computation.3 | async-start | bytes 1310720 | tf_op jit(solution)/shard_map/all_to_all | solution.py:58
Sparse Core Ops, SparseCore 0:
  26.6 95.4 all-gather.1
  193.9 89.8 reduce-scatter.1

commit v2 on v1

v2 whole, which is shorter than its diff:
```python
import functools

import jax
import jax.numpy as jnp
from jax import lax
from jax.experimental import pallas as pl
from jax.experimental.pallas import tpu as pltpu
from jax.sharding import PartitionSpec as P

CAP = 40
F32 = jnp.float32
BF16 = jnp.bfloat16
MESH = pl.DeviceIdType.MESH
LANE = 128


def nt(a, b):
    return lax.dot_general(a, b, (((1,), (1,)), ((), ())), preferred_element_type=F32)


def tn(a, b):
    return lax.dot_general(a, b, (((0,), (0,)), ((), ())), preferred_element_type=F32)


def flat(v):
    return v.astype(F32).reshape(v.shape[0] * v.shape[1], v.shape[2]).astype(BF16)


def blocks(v):
    return v.reshape(v.shape[0] // CAP, CAP, v.shape[1])


def kernel(
    nf, ne, tok_ref, cot_ref, ids_ref, gates_ref, win_hbm, wout_hbm,
    out_ref, ogate_ref, gin_hbm, gout_hbm,
    win, wout, sel32, sel, x2, g2, send_x, x_all, send_g, g_all, pre, gp16, ag16,
    rs_send, rs_recv, back_send, back_recv, pair_send, pair_recv, tok_all,
    gs_send, gs_recv, gf_all, gin, gout,
    load_sem, x_ss, x_rs, g_ss, g_rs, xr_ss, xr_rs, rs_ss, rs_rs, bk_ss, bk_rs,
    pr_ss, pr_rs, tr_ss, tr_rs, gs_ss, gs_rs, gf_ss, gf_rs, st_sem,
):
    me_f, me_e = lax.axis_index("fsdp"), lax.axis_index("expert")
    nz = nf // 2
    lo, z = me_f // nz, me_f % nz
    rows, width = tok_ref.shape
    wz = width // nz
    ff = win.shape[1]
    top = ids_ref.shape[0]
    slots = ne * CAP
    he, hs = ne // 2, slots // 2
    pair_f = (1 - lo) * nz + z
    right_f = lo * nz + (z + 1) % nz
    left_f = lo * nz + (z + nz - 1) % nz

    def dev(f, e):
        return {"fsdp": f, "expert": e}

    def remote(src, dst, ss, rs, f, e):
        return pltpu.make_async_remote_copy(
            src_ref=src, dst_ref=dst, send_sem=ss, recv_sem=rs,
            device_id=dev(f, e), device_id_type=MESH,
        )

    barrier = pltpu.get_barrier_semaphore()

    def greet_e(k, c):
        pl.semaphore_signal(barrier, inc=1, device_id=dev(me_f, (me_e + k) % ne), device_id_type=MESH)
        return c

    def greet_f(k, c):
        pl.semaphore_signal(barrier, inc=1, device_id=dev((me_f + k) % nf, me_e), device_id_type=MESH)
        return c

    lax.fori_loop(1, ne, greet_e, 0)
    lax.fori_loop(1, nf, greet_f, 0)
    load_in = pltpu.make_async_copy(win_hbm, win, load_sem.at[0])
    load_out = pltpu.make_async_copy(wout_hbm, wout, load_sem.at[1])
    load_in.start()
    load_out.start()

    ids = ids_ref[...]
    gates = gates_ref[...].astype(F32)
    exps = lax.broadcasted_iota(jnp.int32, (ne, rows), 0)
    named = jnp.zeros((ne, rows), F32)
    gate_of = jnp.zeros((ne, rows), F32)
    for k in range(top):
        hit = exps == ids[k : k + 1, :]
        named = named + jnp.where(hit, 1.0, 0.0)
        gate_of = gate_of + jnp.where(hit, gates[k : k + 1, :], 0.0)
    before = lax.broadcasted_iota(jnp.int32, (rows, rows), 0) < lax.broadcasted_iota(
        jnp.int32, (rows, rows), 1
    )
    place = jnp.dot(
        named.astype(BF16), jnp.where(before, 1.0, 0.0).astype(BF16), preferred_element_type=F32
    )
    place = jnp.where(named > 0.5, place, -1.0)
    slot_no = lax.broadcasted_iota(jnp.int32, (CAP, rows), 0).astype(F32)
    for e in range(ne):
        one = jnp.where(slot_no == place[e : e + 1, :], 1.0, 0.0)
        sel32[e] = one
        gate_col = jnp.sum(one * gate_of[e : e + 1, :], axis=1, keepdims=True)
        send_g[e, :, width:] = jnp.broadcast_to(gate_col, (CAP, LANE)).astype(BF16)
    sel[...] = sel32[...].reshape(slots, rows).astype(BF16)
    pick = sel[...]
    cols = pl.ds(pl.multiple_of(z * wz, LANE), wz)
    send_x[...] = blocks(jnp.dot(pick, tok_ref[:, cols], preferred_element_type=F32)).astype(BF16)

    pl.semaphore_wait(barrier, (ne - 1) + (nf - 1))

    def x_copy(k):
        e = (me_e + k) % ne
        return remote(send_x.at[e], x_all.at[z, me_e], x_ss.at[e], x_rs.at[me_e], me_f, e)

    def x_start(k, c):
        x_copy(k).start()
        return c

    lax.fori_loop(1, ne, x_start, 0)
    own_x = pltpu.make_async_copy(send_x.at[me_e], x_all.at[z, me_e], st_sem.at[0])
    own_x.start()

    gw = width // 6 if width % (6 * LANE) == 0 else width

    def g_build(j, c):
        span = pl.ds(pl.multiple_of(j * gw, LANE), gw)
        send_g[:, :, span] = blocks(
            jnp.dot(sel[...], cot_ref[:, span], preferred_element_type=F32)
        ).astype(BF16)
        return c

    lax.fori_loop(0, width // gw, g_build, 0)

    def g_start(k, c):
        e = (me_e + k) % ne
        remote(send_g.at[e], g_all.at[me_e], g_ss.at[e], g_rs.at[me_e], me_f, e).start()
        return c

    lax.fori_loop(1, ne, g_start, 0)
    own_g = pltpu.make_async_copy(send_g.at[me_e], g_all.at[me_e], st_sem.at[1])
    own_g.start()

    def x_wait(k, c):
        b = (me_e + ne - k) % ne
        remote(send_x.at[b], x_all.at[z, b], x_ss.at[b], x_rs.at[b], me_f, b).wait_recv()
        return c

    lax.fori_loop(1, ne, x_wait, 0)
    own_x.wait()

    far = nz // 2

    def hops(direction, h):
        return far if direction == h else far - 1

    def ring_copy(buf, lead, ss, rs, direction, h, i):
        piece = (z + nz - i) % nz if direction == 0 else (z + i) % nz
        ref = lead(buf, piece, h)
        return remote(
            ref, ref, ss.at[direction, h, i], rs.at[direction, h, i],
            right_f if direction == 0 else left_f, me_e,
        )

    def ring_arrival(buf, lead, ss, rs, direction, h, i):
        piece = (z + nz - 1 - i) % nz if direction == 0 else (z + 1 + i) % nz
        ref = lead(buf, piece, h)
        return remote(
            ref, ref, ss.at[direction, h, i], rs.at[direction, h, i],
            right_f if direction == 0 else left_f, me_e,
        )

    def ring(buf, lead, ss, rs, between):
        for i in range(far + 1):
            for h in (0, 1):
                for d in (0, 1):
                    if 0 < i <= hops(d, h):
                        ring_arrival(buf, lead, ss, rs, d, h, i - 1).wait_recv()
                    if i < hops(d, h):
                        ring_copy(buf, lead, ss, rs, d, h, i).start()
            between(i)

    def ring_drain(buf, lead, ss, rs):
        for i in range(far):
            for h in (0, 1):
                for d in (0, 1):
                    if i < hops(d, h):
                        ring_copy(buf, lead, ss, rs, d, h, i).wait_send()

    def x_lead(buf, piece, h):
        return buf.at[piece, pl.ds(h * he, he)]

    def add_pre(c):
        w_rows = win[pl.ds(pl.multiple_of(c * wz, LANE), wz), :]
        for h in (0, 1):
            xs = flat(x_all[c, h * he : (h + 1) * he])
            x2[c, h * hs : (h + 1) * hs, :] = xs
            pre[h * hs : (h + 1) * hs, :] += jnp.dot(xs, w_rows, preferred_element_type=F32)

    pre[...] = jnp.zeros_like(pre)

    def x_between(i):
        if i == 0:
            load_in.wait()
            add_pre(z)
            return
        add_pre((z + nz - i) % nz)
        if i < far:
            add_pre((z + i) % nz)

    ring(x_all, x_lead, xr_ss, xr_rs, x_between)

    def g_arrival(b):
        return remote(send_g.at[b], g_all.at[b], g_ss.at[b], g_rs.at[b], me_f, b)

    def g_flat(p):
        g2[pl.ds(pl.multiple_of(p * 2 * CAP, 16), 2 * CAP), :] = flat(
            g_all[pl.ds(2 * p, 2), :, :width]
        )

    own_g.wait()
    g_arrival(me_e + 1 - 2 * (me_e % 2)).wait_recv()
    g_flat(me_e // 2)

    def g_take(k, c):
        p = (me_e // 2 + he - k) % he
        g_arrival(2 * p).wait_recv()
        g_arrival(2 * p + 1).wait_recv()
        g_flat(p)
        return c

    lax.fori_loop(1, he, g_take, 0)
    load_out.wait()

    for h in (0, 1):
        span = slice(h * hs, (h + 1) * hs)
        up = nt(g2[span, :], wout[...])
        gate = g_all[h * he : (h + 1) * he, :, width:].astype(F32).reshape(hs, LANE)
        gate = jnp.concatenate([gate] * (ff // LANE), axis=1)
        p = pre[span, :]
        squash = jax.nn.sigmoid(p)
        active = p * squash
        part = jnp.sum(active * up, axis=1, keepdims=True)
        gs_send[h * he : (h + 1) * he] = blocks(jnp.broadcast_to(part, (hs, LANE)))
        ag16[span, :] = (gate * active).astype(BF16)
        gp16[span, :] = (gate * squash * (1.0 + p * (1.0 - squash)) * up).astype(BF16)

    def share(c, h):
        return blocks(
            nt(gp16[h * hs : (h + 1) * hs, :], win[pl.ds(pl.multiple_of(c * wz, LANE), wz), :])
        )

    def rs_src(d, h, i):
        return rs_send.at[d, h] if i == 0 else rs_recv.at[d, h, i - 1]

    def rs_copy(d, h, i):
        return remote(
            rs_src(d, h, i), rs_recv.at[d, h, i], rs_ss.at[d, h, i], rs_rs.at[d, h, i],
            right_f if d == 0 else left_f, me_e,
        )

    def rs_step(d, h, i):
        n = hops(d, h)
        c = (z + n - i) % nz if d == 0 else (z + nz - (n - i)) % nz
        total = share(c, h)
        if i > 0:
            rs_copy(d, h, i - 1).wait_recv()
            total = total + rs_src(d, h, i)[...].astype(F32)
        rs_src(d, h, i)[...] = total.astype(BF16)
        rs_copy(d, h, i).start()

    def gs_start(k, c):
        e = (me_e + k) % ne
        remote(gs_send.at[e], gs_recv.at[me_e], gs_ss.at[e], gs_rs.at[me_e], me_f, e).start()
        return c

    def gs_wait(k, c):
        b = (me_e + ne - k) % ne
        remote(gs_send.at[b], gs_recv.at[b], gs_ss.at[b], gs_rs.at[b], me_f, b).wait_recv()
        return c

    def grad_in_piece(c):
        gin[pl.ds(pl.multiple_of(c * wz, LANE), wz), :] = tn(
            x2[c], gp16[...]
        ).astype(BF16)

    def grad_out_piece(c):
        span = pl.ds(pl.multiple_of(c * wz, LANE), wz)
        gout[:, span] = tn(
            ag16[...], g2[:, span]
        ).astype(BF16)

    def grads(first, last):
        def one(c, carry):
            grad_in_piece(c)
            grad_out_piece(c)
            return carry

        lax.fori_loop(first, last, one, 0)

    def gates_pass():
        lax.fori_loop(1, ne, gs_wait, 0)
        own_gs.wait()
        acc = jnp.zeros((top, rows), F32)
        for e in range(ne):
            row = jnp.sum(sel32[e] * gs_recv[e], axis=0, keepdims=True)
            acc = acc + jnp.where(ids_ref[...] == e, row, 0.0)
        gf_all[me_f, :top, :] = acc

        def gf_start(k, c):
            f = (me_f + k) % nf
            remote(gf_all.at[me_f], gf_all.at[me_f], gf_ss.at[f], gf_rs.at[me_f], f, me_e).start()
            return c

        lax.fori_loop(1, nf, gf_start, 0)

    own_gs = pltpu.make_async_copy(gs_send.at[me_e], gs_recv.at[me_e], st_sem.at[2])
    for i in range(far):
        for h in (0, 1):
            for d in (0, 1):
                if i < hops(d, h):
                    rs_step(d, h, i)
        if i == 0:
            lax.fori_loop(1, ne, gs_start, 0)
            own_gs.start()
        grads(i * nz // far, (i + 1) * nz // far)
        if i == 0:
            gates_pass()
    store_in = pltpu.make_async_copy(gin, gin_hbm, st_sem.at[3])
    store_out = pltpu.make_async_copy(gout, gout_hbm, st_sem.at[4])
    store_in.start()
    store_out.start()

    def back_start(k, c):
        e = (me_e + k) % ne
        remote(back_send.at[e], back_recv.at[me_e], bk_ss.at[e], bk_rs.at[me_e], me_f, e).start()
        return c

    def back_wait(k, c):
        b = (me_e + ne - k) % ne
        remote(back_send.at[b], back_recv.at[b], bk_ss.at[b], bk_rs.at[b], me_f, b).wait_recv()
        return c

    for h in (0, 1):
        total = share(z, h)
        for d in (0, 1):
            last = hops(d, h) - 1
            rs_copy(d, h, last).wait_recv()
            total = total + rs_recv[d, h, last].astype(F32)
        back_send[h * he : (h + 1) * he] = total.astype(BF16)
    lax.fori_loop(1, ne, back_start, 0)
    own_back = pltpu.make_async_copy(back_send.at[me_e], back_recv.at[me_e], st_sem.at[5])
    own_back.start()

    def gf_wait(k, c):
        f = (me_f + nf - k) % nf
        remote(gf_all.at[f], gf_all.at[f], gf_ss.at[f], gf_rs.at[f], f, me_e).wait_recv()
        return c

    lax.fori_loop(1, nf, gf_wait, 0)
    total_gate = gf_all[0, :top, :]
    for f in range(1, nf):
        total_gate = total_gate + gf_all[f, :top, :]
    ogate_ref[...] = total_gate.astype(BF16)

    lax.fori_loop(1, ne, back_wait, 0)
    own_back.wait()
    tok = tn(sel[...], flat(back_recv[...]))
    pair_send[...] = tok.astype(BF16)
    pair = remote(pair_send, pair_recv, pr_ss, pr_rs, pair_f, me_e)
    pair.start()
    pair.wait_recv()
    tok_all[z] = (pair_send[...].astype(F32) + pair_recv[...].astype(F32)).astype(BF16)

    hr = rows // 2

    def t_lead(buf, piece, h):
        return buf.at[piece, pl.ds(h * hr, hr)]

    ring(tok_all, t_lead, tr_ss, tr_rs, lambda i: None)
    for c in range(nz):
        out_ref[:, c * wz : (c + 1) * wz] = tok_all[c]

    def drain(k, c):
        e = (me_e + k) % ne
        remote(send_x.at[e], x_all.at[z, me_e], x_ss.at[e], x_rs.at[me_e], me_f, e).wait_send()
        remote(send_g.at[e], g_all.at[me_e], g_ss.at[e], g_rs.at[me_e], me_f, e).wait_send()
        remote(gs_send.at[e], gs_recv.at[me_e], gs_ss.at[e], gs_rs.at[me_e], me_f, e).wait_send()
        remote(back_send.at[e], back_recv.at[me_e], bk_ss.at[e], bk_rs.at[me_e], me_f, e).wait_send()
        return c

    def drain_f(k, c):
        f = (me_f + k) % nf
        remote(gf_all.at[me_f], gf_all.at[me_f], gf_ss.at[f], gf_rs.at[me_f], f, me_e).wait_send()
        return c

    lax.fori_loop(1, ne, drain, 0)
    lax.fori_loop(1, nf, drain_f, 0)
    ring_drain(x_all, x_lead, xr_ss, xr_rs)
    ring_drain(tok_all, t_lead, tr_ss, tr_rs)
    for i in range(far):
        for h in (0, 1):
            for d in (0, 1):
                if i < hops(d, h):
                    rs_copy(d, h, i).wait_send()
    pair.wait_send()
    store_in.wait()
    store_out.wait()


def local(nf, ne, tokens, cotangent, expert_ids, gate_values, w_in, w_out):
    rows, width = tokens.shape
    top = expert_ids.shape[1]
    ff = w_in.shape[2]
    nz = nf // 2
    wz = width // nz
    far = nz // 2
    he = ne // 2
    dma = pltpu.SemaphoreType.DMA
    vmem = pl.BlockSpec(memory_space=pltpu.VMEM)
    hbm = pl.BlockSpec(memory_space=pl.ANY)
    ring_sems = dma((2, 2, far))
    out = pl.pallas_call(
        functools.partial(kernel, nf, ne),
        out_shape=(
            jax.ShapeDtypeStruct((rows, width), BF16),
            jax.ShapeDtypeStruct((top, rows), BF16),
            jax.ShapeDtypeStruct((width, ff), BF16),
            jax.ShapeDtypeStruct((ff, width), BF16),
        ),
        in_specs=[vmem, vmem, vmem, vmem, hbm, hbm],
        out_specs=(vmem, vmem, hbm, hbm),
        scratch_shapes=[
            pltpu.VMEM((width, ff), BF16),
            pltpu.VMEM((ff, width), BF16),
            pltpu.VMEM((ne, CAP, rows), F32),
            pltpu.VMEM((ne * CAP, rows), BF16),
            pltpu.VMEM((nz, ne * CAP, wz), BF16),
            pltpu.VMEM((ne * CAP, width), BF16),
            pltpu.VMEM((ne, CAP, wz), BF16),
            pltpu.VMEM((nz, ne, CAP, wz), BF16),
            pltpu.VMEM((ne, CAP, width + LANE), BF16),
            pltpu.VMEM((ne, CAP, width + LANE), BF16),
            pltpu.VMEM((ne * CAP, ff), F32),
            pltpu.VMEM((ne * CAP, ff), BF16),
            pltpu.VMEM((ne * CAP, ff), BF16),
            pltpu.VMEM((2, 2, he, CAP, wz), BF16),
            pltpu.VMEM((2, 2, far, he, CAP, wz), BF16),
            pltpu.VMEM((ne, CAP, wz), BF16),
            pltpu.VMEM((ne, CAP, wz), BF16),
            pltpu.VMEM((rows, wz), BF16),
            pltpu.VMEM((rows, wz), BF16),
            pltpu.VMEM((nz, rows, wz), BF16),
            pltpu.VMEM((ne, CAP, LANE), F32),
            pltpu.VMEM((ne, CAP, LANE), F32),
            pltpu.VMEM((nf, 8, rows), F32),
            pltpu.VMEM((width, ff), BF16),
            pltpu.VMEM((ff, width), BF16),
            dma((2,)),
            dma((ne,)), dma((ne,)), dma((ne,)), dma((ne,)),
            ring_sems, ring_sems, ring_sems, ring_sems,
            dma((ne,)), dma((ne,)),
            dma, dma,
            ring_sems, ring_sems,
            dma((ne,)), dma((ne,)),
            dma((nf,)), dma((nf,)),
            dma((6,)),
        ],
        compiler_params=pltpu.CompilerParams(
            collective_id=0, has_side_effects=True, vmem_limit_bytes=62 * 1024 * 1024
        ),
    )(
        tokens, cotangent, expert_ids.T, gate_values.T,
        w_in.reshape(width, ff), w_out.reshape(ff, width),
    )
    return (
        out[0],
        out[1].T,
        out[2].reshape(w_in.shape),
        out[3].reshape(w_out.shape),
    )


def solution(mesh):
    return jax.shard_map(
        functools.partial(local, mesh.shape["fsdp"], mesh.shape["expert"]),
        mesh=mesh,
        in_specs=(
            P("expert", None),
            P("expert", None),
            P("expert", None),
            P("expert", None),
            P(None, "expert", "fsdp"),
            P("fsdp", "expert", None),
        ),
        out_specs=(
            P("expert", None),
            P("expert", None),
            P(None, "expert", "fsdp"),
            P("fsdp", "expert", None),
        ),
        check_vma=False,
    )
```

time: 351 us -> 150 us (0.43)
  waiting for transfers between devices: 181 us -> 0 us
  Pallas kernels: 0 us -> 140 us
  blocking collectives: 96.2 us -> 0 us
  matrix products: 26.2 us -> 0 us
  starting transfers between devices: 14.6 us -> 0 us
  between operations: 14.2 us -> 0.64 us
  local copies, waits for them, and re-layouts: 12.7 us -> 8.12 us
  other arithmetic: 4.41 us -> 0 us
    pallas_call x0 -> x1, Pallas kernels: none -> 140 us  [local(): pl.pallas_call(functools.partial(kernel, nf, ne), out_shape=(jax.ShapeDty...]
    all_gather x1 -> x0, waiting for transfers between devices: 92 us -> none  [local(): every = lax.all_gather(got.reshape(EXPERTS * CAP, part), 'fsdp', axis=0)]
    reduce_scatter x1 -> x0, waiting for transfers between devices: 78.9 us -> none  [local(): mine = lax.psum_scatter(part_x, 'fsdp', scatter_dimension=0, tiled=False)]
    all_gather x1 -> x0, blocking collectives: 35.9 us -> none  [local(): grad_tokens = lax.all_gather(tok, 'fsdp', axis=1, tiled=True)]
    psum x1 -> x0, blocking collectives: 33.5 us -> none  [local(): gate_sum = lax.psum(gate_part.reshape(EXPERTS, CAP), 'fsdp')]
    all_to_all x2 -> x0, blocking collectives: 26.8 us -> none  [the longest x1 16.7 us: local(): lax.all_to_all(send, 'expert', split_axis=0, concat_axis=0, tiled=True)]
    dot_general x8 -> x0, matrix products: 26.2 us -> none  [the longest x1 6.3 us: local(): jnp.einsum('sf,zsd->fzd', act_gated, gs, preferred_element_type=F32)]
    all_to_all x2 -> x0, starting transfers between devices: 14.6 us -> none  [the longest x1 7.28 us: local(): lax.all_to_all(mine.reshape(EXPERTS, CAP, -1), 'expert', 0, 0, tiled=True)]
  transfers between devices with their start and end apart: 4 -> 0, of which waited for: 4 -> 0; matrix products, arithmetic and copies ran while one was open for 6% -> 0% of each run, Pallas kernels for 0% -> 0%
where the time goes in v2:
time: 150 us; the launch traced here: 148 us
  Pallas kernels  140 us (93%)
  local copies, waits for them, and re-layouts  8.12 us (5%)
    pallas_call x1, Pallas kernels, local(): pl.pallas_call(functools.partial(kernel, nf, ne), out_shape=(jax.ShapeDty...  140 us
    unnamed x6, local copies, waits for them, and re-layouts  8.12 us

profile of v2, /device:TPU:6, one launch (start us, length us, event | category | flops | bytes accessed | tf_op | source)
XLA Modules:
  0.0 148.4 jit_solution(515399650038581438)
XLA Ops:
  0.6 139.7 %shard_map.93 = (bf16[128,3072]{1,0:T(8,128)(2,1)}, bf16[4,128]{1,0:T(4,128)(2,1)}, bf16[3072,384]{1,0:T(8,128)(2,1)}, bf16[384,3072]{1,0:T(8,128)(2,1)}) custom-call(bf16[128,3072]{1,0:T(8,128)(2,1)} %tok_ref.1, bf16[128,3072]{1,0:T(8,128)(2,1)} %cot_ref.1, s32[4,128]{1,0:T(4,128)} %bitcast.11, bf16[4,128]{1,0:T(4,128)(2,1)} %bitcast.12, ...), custom_call_target="tpu_custom_call" | custom-call | tf_op jit(solution)/shard_map/pallas_call | solution.py:421
  140.3 2.1 %copy.14 = bf16[128,3072]{1,0:T(8,128)(2,1)} copy(bf16[128,3072]{1,0:T(8,128)(2,1)} %get-tuple-element.16) | data formatting | bytes 1572864
  142.4 1.2 copy.15
  143.6 0.0 copy-start
  143.6 3.5 %copy.16 = bf16[3072,1,384]{2,0,1:T(8,128)(2,1)} copy(bf16[3072,1,384]{2,0,1:T(8,128)(2,1)} %bitcast.10) | data formatting | bytes 4718592
  147.0 0.0 copy-done
  147.0 1.4 copy.17
Async XLA Ops:
  143.6 3.5 %copy-start = (bf16[384,3072]{1,0:T(8,128)(2,1)S(1)}, bf16[384,3072]{1,0:T(8,128)(2,1)}, u32[]{:S(2)}) copy-start(bf16[384,3072]{1,0:T(8,128)(2,1)} %get-tuple-element.11) | copy-start | bytes 7077892

commit v3 on v2

--- a/solution.py
+++ b/solution.py
@@ -12,6 +12,7 @@
 BF16 = jnp.bfloat16
 MESH = pl.DeviceIdType.MESH
 LANE = 128
+PIECES = 4
 
 
 def nt(a, b):
@@ -37,7 +38,7 @@
     rs_send, rs_recv, back_send, back_recv, pair_send, pair_recv, tok_all,
     gs_send, gs_recv, gf_all, gin, gout,
     load_sem, x_ss, x_rs, g_ss, g_rs, xr_ss, xr_rs, rs_ss, rs_rs, bk_ss, bk_rs,
-    pr_ss, pr_rs, tr_ss, tr_rs, gs_ss, gs_rs, gf_ss, gf_rs, st_sem,
+    pr_ss, pr_rs, tr_ss, tr_rs, gs_ss, gs_rs, gf_ss, gf_rs, fw_ss, fw_rs, st_sem,
 ):
     me_f, me_e = lax.axis_index("fsdp"), lax.axis_index("expert")
     nz = nf // 2
@@ -49,6 +50,9 @@
     slots = ne * CAP
     he, hs = ne // 2, slots // 2
     pair_f = (1 - lo) * nz + z
+    wl = width // LANE // 3 * LANE
+    wn = width - wl
+    wm = wn + LANE
     right_f = lo * nz + (z + 1) % nz
     left_f = lo * nz + (z + nz - 1) % nz
 
@@ -61,10 +65,17 @@
             device_id=dev(f, e), device_id_type=MESH,
         )
 
+    def near(e):
+        return (lo + (e // 2) % 2 + (me_e // 2) % 2) % 2
+
+    def near_f(e):
+        return near(e) * nz + z
+
     barrier = pltpu.get_barrier_semaphore()
 
     def greet_e(k, c):
-        pl.semaphore_signal(barrier, inc=1, device_id=dev(me_f, (me_e + k) % ne), device_id_type=MESH)
+        e = (me_e + k) % ne
+        pl.semaphore_signal(barrier, inc=1, device_id=dev(near_f(e), e), device_id_type=MESH)
         return c
 
     def greet_f(k, c):
@@ -99,7 +110,7 @@
         one = jnp.where(slot_no == place[e : e + 1, :], 1.0, 0.0)
         sel32[e] = one
         gate_col = jnp.sum(one * gate_of[e : e + 1, :], axis=1, keepdims=True)
-        send_g[e, :, width:] = jnp.broadcast_to(gate_col, (CAP, LANE)).astype(BF16)
+        send_g[e, :, wn : wn + LANE] = jnp.broadcast_to(gate_col, (CAP, LANE)).astype(BF16)
     sel[...] = sel32[...].reshape(slots, rows).astype(BF16)
     pick = sel[...]
     cols = pl.ds(pl.multiple_of(z * wz, LANE), wz)
@@ -109,7 +120,7 @@
 
     def x_copy(k):
         e = (me_e + k) % ne
-        return remote(send_x.at[e], x_all.at[z, me_e], x_ss.at[e], x_rs.at[me_e], me_f, e)
+        return remote(send_x.at[e], x_all.at[z, me_e], x_ss.at[e], x_rs.at[me_e], near_f(e), e)
 
     def x_start(k, c):
         x_copy(k).start()
@@ -119,20 +130,40 @@
     own_x = pltpu.make_async_copy(send_x.at[me_e], x_all.at[z, me_e], st_sem.at[0])
     own_x.start()
 
-    gw = width // 6 if width % (6 * LANE) == 0 else width
+    gw = 4 * LANE if wl % (4 * LANE) == 0 and wn % (4 * LANE) == 0 else LANE
 
     def g_build(j, c):
-        span = pl.ds(pl.multiple_of(j * gw, LANE), gw)
-        send_g[:, :, span] = blocks(
-            jnp.dot(sel[...], cot_ref[:, span], preferred_element_type=F32)
+        src = pl.ds(pl.multiple_of(j * gw, LANE), gw)
+        dst = pl.ds(pl.multiple_of(j * gw + j // (wn // gw) * LANE, LANE), gw)
+        send_g[:, :, dst] = blocks(
+            jnp.dot(sel[...], cot_ref[:, src], preferred_element_type=F32)
         ).astype(BF16)
         return c
 
     lax.fori_loop(0, width // gw, g_build, 0)
 
+    def g_part(side):
+        return pl.ds(pl.multiple_of(side * wl, LANE), wm)
+
+    def g_copy(e):
+        part = g_part(near(e))
+        return remote(
+            send_g.at[e, :, part], g_all.at[me_e, :, part], g_ss.at[e], g_rs.at[me_e], near_f(e), e
+        )
+
+    def g_arrival(b):
+        part = g_part(lo)
+        return remote(
+            send_g.at[b, :, part], g_all.at[b, :, part], g_ss.at[b], g_rs.at[b], near_f(b), b
+        )
+
+    def fw_copy(b, side):
+        part = pl.ds(pl.multiple_of(side * wm, LANE), wl)
+        ref = g_all.at[b, :, part]
+        return remote(ref, ref, fw_ss.at[b], fw_rs.at[b], pair_f, me_e)
+
     def g_start(k, c):
-        e = (me_e + k) % ne
-        remote(send_g.at[e], g_all.at[me_e], g_ss.at[e], g_rs.at[me_e], me_f, e).start()
+        g_copy((me_e + k) % ne).start()
         return c
 
     lax.fori_loop(1, ne, g_start, 0)
@@ -141,7 +172,7 @@
 
     def x_wait(k, c):
         b = (me_e + ne - k) % ne
-        remote(send_x.at[b], x_all.at[z, b], x_ss.at[b], x_rs.at[b], me_f, b).wait_recv()
+        remote(send_x.at[b], x_all.at[z, b], x_ss.at[b], x_rs.at[b], near_f(b), b).wait_recv()
         return c
 
     lax.fori_loop(1, ne, x_wait, 0)
@@ -197,7 +228,19 @@
 
     pre[...] = jnp.zeros_like(pre)
 
+    order = list(range(1, ne))
+    if ne == 16:
+        order = [1, 2, 3, 4, 12, 5, 13, 6, 14, 7, 15, 8, 9, 10, 11]
+
+    def forward(i):
+        n = len(order)
+        for k in order[n * i // (far + 1) : n * (i + 1) // (far + 1)]:
+            b = (me_e + ne - k) % ne
+            g_arrival(b).wait_recv()
+            fw_copy(b, lo).start()
+
     def x_between(i):
+        forward(i)
         if i == 0:
             load_in.wait()
             add_pre(z)
@@ -208,22 +251,20 @@
 
     ring(x_all, x_lead, xr_ss, xr_rs, x_between)
 
-    def g_arrival(b):
-        return remote(send_g.at[b], g_all.at[b], g_ss.at[b], g_rs.at[b], me_f, b)
-
     def g_flat(p):
-        g2[pl.ds(pl.multiple_of(p * 2 * CAP, 16), 2 * CAP), :] = flat(
-            g_all[pl.ds(2 * p, 2), :, :width]
-        )
+        at = pl.ds(pl.multiple_of(p * 2 * CAP, 16), 2 * CAP)
+        two = pl.ds(2 * p, 2)
+        g2[at, :wn] = flat(g_all[two, :, :wn])
+        g2[at, wn:] = flat(g_all[two, :, wn + LANE :])
 
     own_g.wait()
-    g_arrival(me_e + 1 - 2 * (me_e % 2)).wait_recv()
+    fw_copy(me_e + 1 - 2 * (me_e % 2), 1 - lo).wait_recv()
     g_flat(me_e // 2)
 
     def g_take(k, c):
         p = (me_e // 2 + he - k) % he
-        g_arrival(2 * p).wait_recv()
-        g_arrival(2 * p + 1).wait_recv()
+        fw_copy(2 * p, 1 - lo).wait_recv()
+        fw_copy(2 * p + 1, 1 - lo).wait_recv()
         g_flat(p)
         return c
 
@@ -233,7 +274,7 @@
     for h in (0, 1):
         span = slice(h * hs, (h + 1) * hs)
         up = nt(g2[span, :], wout[...])
-        gate = g_all[h * he : (h + 1) * he, :, width:].astype(F32).reshape(hs, LANE)
+        gate = g_all[h * he : (h + 1) * he, :, wn : wn + LANE].astype(F32).reshape(hs, LANE)
         gate = jnp.concatenate([gate] * (ff // LANE), axis=1)
         p = pre[span, :]
         squash = jax.nn.sigmoid(p)
@@ -269,12 +310,12 @@
 
     def gs_start(k, c):
         e = (me_e + k) % ne
-        remote(gs_send.at[e], gs_recv.at[me_e], gs_ss.at[e], gs_rs.at[me_e], me_f, e).start()
+        remote(gs_send.at[e], gs_recv.at[me_e], gs_ss.at[e], gs_rs.at[me_e], near_f(e), e).start()
         return c
 
     def gs_wait(k, c):
         b = (me_e + ne - k) % ne
-        remote(gs_send.at[b], gs_recv.at[b], gs_ss.at[b], gs_rs.at[b], me_f, b).wait_recv()
+        remote(gs_send.at[b], gs_recv.at[b], gs_ss.at[b], gs_rs.at[b], near_f(b), b).wait_recv()
         return c
 
     def grad_in_piece(c):
@@ -331,12 +372,12 @@
 
     def back_start(k, c):
         e = (me_e + k) % ne
-        remote(back_send.at[e], back_recv.at[me_e], bk_ss.at[e], bk_rs.at[me_e], me_f, e).start()
+        remote(back_send.at[e], back_recv.at[me_e], bk_ss.at[e], bk_rs.at[me_e], near_f(e), e).start()
         return c
 
     def back_wait(k, c):
         b = (me_e + ne - k) % ne
-        remote(back_send.at[b], back_recv.at[b], bk_ss.at[b], bk_rs.at[b], me_f, b).wait_recv()
+        remote(back_send.at[b], back_recv.at[b], bk_ss.at[b], bk_rs.at[b], near_f(b), b).wait_recv()
         return c
 
     for h in (0, 1):
@@ -364,11 +405,11 @@
     lax.fori_loop(1, ne, back_wait, 0)
     own_back.wait()
     tok = tn(sel[...], flat(back_recv[...]))
-    pair_send[...] = tok.astype(BF16)
+    pair_send[...] = tok
     pair = remote(pair_send, pair_recv, pr_ss, pr_rs, pair_f, me_e)
     pair.start()
     pair.wait_recv()
-    tok_all[z] = (pair_send[...].astype(F32) + pair_recv[...].astype(F32)).astype(BF16)
+    tok_all[z] = (pair_send[...] + pair_recv[...]).astype(BF16)
 
     hr = rows // 2
 
@@ -381,10 +422,11 @@
 
     def drain(k, c):
         e = (me_e + k) % ne
-        remote(send_x.at[e], x_all.at[z, me_e], x_ss.at[e], x_rs.at[me_e], me_f, e).wait_send()
-        remote(send_g.at[e], g_all.at[me_e], g_ss.at[e], g_rs.at[me_e], me_f, e).wait_send()
-        remote(gs_send.at[e], gs_recv.at[me_e], gs_ss.at[e], gs_rs.at[me_e], me_f, e).wait_send()
-        remote(back_send.at[e], back_recv.at[me_e], bk_ss.at[e], bk_rs.at[me_e], me_f, e).wait_send()
+        x_copy(k).wait_send()
+        g_copy(e).wait_send()
+        fw_copy(e, lo).wait_send()
+        remote(gs_send.at[e], gs_recv.at[me_e], gs_ss.at[e], gs_rs.at[me_e], near_f(e), e).wait_send()
+        remote(back_send.at[e], back_recv.at[me_e], bk_ss.at[e], bk_rs.at[me_e], near_f(e), e).wait_send()
         return c
 
     def drain_f(k, c):
@@ -404,6 +446,26 @@
     pair.wait_send()
     store_in.wait()
     store_out.wait()
+
+
+def passing(a0, a1, a2, a3, o0, o1, o2, o3, b0, b1, b2, b3, sems):
+    moves = []
+    for n, (a, o, b) in enumerate(((a0, o0, b0), (a1, o1, b1), (a2, o2, b2), (a3, o3, b3))):
+        pieces = PIECES if n > 1 else 1
+        step = a.shape[0] // pieces
+        for p in range(pieces):
+            at = pl.ds(p * step, step)
+            moves.append((
+                pltpu.make_async_copy(a.at[at], b.at[at], sems.at[0, n, p]),
+                pltpu.make_async_copy(b.at[at], o.at[at], sems.at[1, n, p]),
+            ))
+    for get, _ in moves:
+        get.start()
+    for get, put in moves:
+        get.wait()
+        put.start()
+    for _, put in moves:
+        put.wait()
 
 
 def local(nf, ne, tokens, cotangent, expert_ids, gate_values, w_in, w_out):
@@ -446,8 +508,8 @@
             pltpu.VMEM((2, 2, far, he, CAP, wz), BF16),
             pltpu.VMEM((ne, CAP, wz), BF16),
             pltpu.VMEM((ne, CAP, wz), BF16),
-            pltpu.VMEM((rows, wz), BF16),
-            pltpu.VMEM((rows, wz), BF16),
+            pltpu.VMEM((rows, wz), F32),
+            pltpu.VMEM((rows, wz), F32),
             pltpu.VMEM((nz, rows, wz), BF16),
             pltpu.VMEM((ne, CAP, LANE), F32),
             pltpu.VMEM((ne, CAP, LANE), F32),
@@ -462,6 +524,7 @@
             ring_sems, ring_sems,
             dma((ne,)), dma((ne,)),
             dma((nf,)), dma((nf,)),
+            dma((ne,)), dma((ne,)),
             dma((6,)),
         ],
         compiler_params=pltpu.CompilerParams(
@@ -471,6 +534,14 @@
         tokens, cotangent, expert_ids.T, gate_values.T,
         w_in.reshape(width, ff), w_out.reshape(ff, width),
     )
+    out = pl.pallas_call(
+        passing,
+        out_shape=tuple(jax.ShapeDtypeStruct(a.shape, a.dtype) for a in out),
+        in_specs=[hbm] * 4,
+        out_specs=(hbm,) * 4,
+        scratch_shapes=[pltpu.VMEM(a.shape, a.dtype) for a in out] + [dma((2, 4, PIECES))],
+        compiler_params=pltpu.CompilerParams(vmem_limit_bytes=62 * 1024 * 1024),
+    )(*out)
     return (
         out[0],
         out[1].T,

time: 150 us -> 155 us (1.033)
  Pallas kernels: 140 us -> 153 us
  local copies, waits for them, and re-layouts: 8.12 us -> 0 us
    pallas_call x1, Pallas kernels: 140 us -> 148 us  [local(): pl.pallas_call(functools.partial(kernel, nf, ne), out_shape=(jax.ShapeDty...]
    unnamed x6 -> x0, local copies, waits for them, and re-layouts: 8.12 us -> none
    pallas_call x0 -> x1, Pallas kernels: none -> 4.9 us  [local(): pl.pallas_call(passing, out_shape=tuple((jax.ShapeDtypeStruct(a.shape, a....]
where the time goes in v3:
time: 155 us; the launch traced here: 154 us
  Pallas kernels  153 us (99%)
    pallas_call x1, Pallas kernels, local(): pl.pallas_call(functools.partial(kernel, nf, ne), out_shape=(jax.ShapeDty...  148 us
    pallas_call x1, Pallas kernels, local(): pl.pallas_call(passing, out_shape=tuple((jax.ShapeDtypeStruct(a.shape, a....  4.9 us

profile of v3, /device:TPU:6, one launch (start us, length us, event | category | flops | bytes accessed | tf_op | source)
XLA Modules:
  0.0 153.6 jit_solution(9926039106105594298)
XLA Ops:
  0.6 148.1 %shard_map.93 = (bf16[128,3072]{1,0:T(8,128)(2,1)}, bf16[4,128]{1,0:T(4,128)(2,1)}, bf16[3072,384]{1,0:T(8,128)(2,1)}, bf16[384,3072]{1,0:T(8,128)(2,1)}) custom-call(bf16[128,3072]{1,0:T(8,128)(2,1)} %tok_ref.1, bf16[128,3072]{1,0:T(8,128)(2,1)} %cot_ref.1, s32[4,128]{1,0:T(4,128)} %bitcast.9, bf16[4,128]{1,0:T(4,128)(2,1)} %bitcast.10, ...), custom_call_target="tpu_custom_call" | custom-call | tf_op jit(solution)/shard_map/pallas_call | solution.py:483
  148.7 4.9 %shard_map.94 = (bf16[128,3072]{1,0:T(8,128)(2,1)}, bf16[4,128]{1,0:T(4,128)(2,1)}, bf16[3072,384]{1,0:T(8,128)(2,1)}, bf16[384,3072]{1,0:T(8,128)(2,1)}) custom-call(bf16[128,3072]{1,0:T(8,128)(2,1)} %get-tuple-element.12.a0, bf16[4,128]{1,0:T(4,128)(2,1)} %get-tuple-element.13.a1, bf16[3072,384]{1,0:T(8,128)(2,1)} %get-tuple-element.14.a2, ...), custom_call_target="tpu_custom_call" | custom-call | tf_op jit(solution)/shard_map/pallas_call | solution.py:537

commit v4 on v2

--- a/solution.py
+++ b/solution.py
@@ -12,6 +12,7 @@
 BF16 = jnp.bfloat16
 MESH = pl.DeviceIdType.MESH
 LANE = 128
+PIECES = 4
 
 
 def nt(a, b):
@@ -35,9 +36,9 @@
     out_ref, ogate_ref, gin_hbm, gout_hbm,
     win, wout, sel32, sel, x2, g2, send_x, x_all, send_g, g_all, pre, gp16, ag16,
     rs_send, rs_recv, back_send, back_recv, pair_send, pair_recv, tok_all,
-    gs_send, gs_recv, gf_all, gin, gout,
+    gs_send, gs_recv, gf_all, gin, gout, d_send, d_recv, ts_send, ts_recv,
     load_sem, x_ss, x_rs, g_ss, g_rs, xr_ss, xr_rs, rs_ss, rs_rs, bk_ss, bk_rs,
-    pr_ss, pr_rs, tr_ss, tr_rs, gs_ss, gs_rs, gf_ss, gf_rs, st_sem,
+    pr_ss, pr_rs, tr_ss, tr_rs, gs_ss, gs_rs, gf_ss, gf_rs, d_ss, d_rs, ts_ss, ts_rs, st_sem,
 ):
     me_f, me_e = lax.axis_index("fsdp"), lax.axis_index("expert")
     nz = nf // 2
@@ -48,6 +49,8 @@
     top = ids_ref.shape[0]
     slots = ne * CAP
     he, hs = ne // 2, slots // 2
+    sub = LANE
+    wr = wz - sub
     pair_f = (1 - lo) * nz + z
     right_f = lo * nz + (z + 1) % nz
     left_f = lo * nz + (z + nz - 1) % nz
@@ -244,9 +247,53 @@
         gp16[span, :] = (gate * squash * (1.0 + p * (1.0 - squash)) * up).astype(BF16)
 
     def share(c, h):
-        return blocks(
-            nt(gp16[h * hs : (h + 1) * hs, :], win[pl.ds(pl.multiple_of(c * wz, LANE), wz), :])
-        )
+        part = win[pl.ds(pl.multiple_of(c * wz + sub, LANE), wr), :]
+        return blocks(nt(gp16[h * hs : (h + 1) * hs, :], part))
+
+    def direct_build(c, carry):
+        part = win[pl.ds(pl.multiple_of(c * wz, LANE), sub), :]
+        d_send[:, :, pl.ds(pl.multiple_of(c * sub, LANE), sub)] = blocks(
+            nt(gp16[...], part)
+        ).astype(BF16)
+        return carry
+
+    def d_start(k, c):
+        e = (me_e + k) % ne
+        remote(d_send.at[e], d_recv.at[me_e], d_ss.at[e], d_rs.at[me_e], me_f, e).start()
+        return c
+
+    def d_wait(k, c):
+        b = (me_e + ne - k) % ne
+        remote(d_send.at[b], d_recv.at[b], d_ss.at[b], d_rs.at[b], me_f, b).wait_recv()
+        return c
+
+    def t_start(k, c):
+        o = (z + k) % nz
+        remote(
+            ts_send.at[o], ts_recv.at[z], ts_ss.at[o], ts_rs.at[z], lo * nz + o, me_e
+        ).start()
+        return c
+
+    def t_wait(k, c):
+        o = (z + nz - k) % nz
+        remote(
+            ts_send.at[o], ts_recv.at[o], ts_ss.at[o], ts_rs.at[o], lo * nz + o, me_e
+        ).wait_recv()
+        return c
+
+    def direct_combine():
+        lax.fori_loop(1, ne, d_wait, 0)
+        own_d.wait()
+
+        def one(c, carry):
+            part = flat(d_recv[:, :, pl.ds(pl.multiple_of(c * sub, LANE), sub)])
+            ts_send[c] = tn(sel[...], part).astype(BF16)
+            return carry
+
+        lax.fori_loop(0, nz, one, 0)
+        lax.fori_loop(1, nz, t_start, 0)
+
+    own_d = pltpu.make_async_copy(d_send.at[me_e], d_recv.at[me_e], st_sem.at[6])
 
     def rs_src(d, h, i):
         return rs_send.at[d, h] if i == 0 else rs_recv.at[d, h, i - 1]
@@ -321,9 +368,14 @@
         if i == 0:
             lax.fori_loop(1, ne, gs_start, 0)
             own_gs.start()
+            lax.fori_loop(0, nz, direct_build, 0)
+            lax.fori_loop(1, ne, d_start, 0)
+            own_d.start()
         grads(i * nz // far, (i + 1) * nz // far)
         if i == 0:
             gates_pass()
+        if i == max(far - 2, 0):
+            direct_combine()
     store_in = pltpu.make_async_copy(gin, gin_hbm, st_sem.at[3])
     store_out = pltpu.make_async_copy(gout, gout_hbm, st_sem.at[4])
     store_in.start()
@@ -361,14 +413,20 @@
         total_gate = total_gate + gf_all[f, :top, :]
     ogate_ref[...] = total_gate.astype(BF16)
 
+    lax.fori_loop(1, nz, t_wait, 0)
+    total = ts_send[z].astype(F32)
+    for k in range(1, nz):
+        total = total + ts_recv[(z + k) % nz].astype(F32)
+    pair_send[:, :sub] = total
+
     lax.fori_loop(1, ne, back_wait, 0)
     own_back.wait()
     tok = tn(sel[...], flat(back_recv[...]))
-    pair_send[...] = tok.astype(BF16)
+    pair_send[:, sub:] = tok
     pair = remote(pair_send, pair_recv, pr_ss, pr_rs, pair_f, me_e)
     pair.start()
     pair.wait_recv()
-    tok_all[z] = (pair_send[...].astype(F32) + pair_recv[...].astype(F32)).astype(BF16)
+    tok_all[z] = (pair_send[...] + pair_recv[...]).astype(BF16)
 
     hr = rows // 2
 
@@ -384,6 +442,7 @@
         remote(send_x.at[e], x_all.at[z, me_e], x_ss.at[e], x_rs.at[me_e], me_f, e).wait_send()
         remote(send_g.at[e], g_all.at[me_e], g_ss.at[e], g_rs.at[me_e], me_f, e).wait_send()
         remote(gs_send.at[e], gs_recv.at[me_e], gs_ss.at[e], gs_rs.at[me_e], me_f, e).wait_send()
+        remote(d_send.at[e], d_recv.at[me_e], d_ss.at[e], d_rs.at[me_e], me_f, e).wait_send()
         remote(back_send.at[e], back_recv.at[me_e], bk_ss.at[e], bk_rs.at[me_e], me_f, e).wait_send()
         return c
 
@@ -394,6 +453,15 @@
 
     lax.fori_loop(1, ne, drain, 0)
     lax.fori_loop(1, nf, drain_f, 0)
+
+    def drain_z(k, c):
+        o = (z + k) % nz
+        remote(
+            ts_send.at[o], ts_recv.at[z], ts_ss.at[o], ts_rs.at[z], lo * nz + o, me_e
+        ).wait_send()
+        return c
+
+    lax.fori_loop(1, nz, drain_z, 0)
     ring_drain(x_all, x_lead, xr_ss, xr_rs)
     ring_drain(tok_all, t_lead, tr_ss, tr_rs)
     for i in range(far):
@@ -404,6 +472,26 @@
     pair.wait_send()
     store_in.wait()
     store_out.wait()
+
+
+def passing(a0, a1, a2, a3, o0, o1, o2, o3, b0, b1, b2, b3, sems):
+    moves = []
+    for n, (a, o, b) in enumerate(((a0, o0, b0), (a1, o1, b1), (a2, o2, b2), (a3, o3, b3))):
+        pieces = PIECES if n > 1 else 1
+        step = a.shape[0] // pieces
+        for p in range(pieces):
+            at = pl.ds(p * step, step)
+            moves.append((
+                pltpu.make_async_copy(a.at[at], b.at[at], sems.at[0, n, p]),
+                pltpu.make_async_copy(b.at[at], o.at[at], sems.at[1, n, p]),
+            ))
+    for get, _ in moves:
+        get.start()
+    for get, put in moves:
+        get.wait()
+        put.start()
+    for _, put in moves:
+        put.wait()
 
 
 def local(nf, ne, tokens, cotangent, expert_ids, gate_values, w_in, w_out):
@@ -442,18 +530,22 @@
             pltpu.VMEM((ne * CAP, ff), F32),
             pltpu.VMEM((ne * CAP, ff), BF16),
             pltpu.VMEM((ne * CAP, ff), BF16),
-            pltpu.VMEM((2, 2, he, CAP, wz), BF16),
-            pltpu.VMEM((2, 2, far, he, CAP, wz), BF16),
-            pltpu.VMEM((ne, CAP, wz), BF16),
-            pltpu.VMEM((ne, CAP, wz), BF16),
-            pltpu.VMEM((rows, wz), BF16),
-            pltpu.VMEM((rows, wz), BF16),
+            pltpu.VMEM((2, 2, he, CAP, wz - LANE), BF16),
+            pltpu.VMEM((2, 2, far, he, CAP, wz - LANE), BF16),
+            pltpu.VMEM((ne, CAP, wz - LANE), BF16),
+            pltpu.VMEM((ne, CAP, wz - LANE), BF16),
+            pltpu.VMEM((rows, wz), F32),
+            pltpu.VMEM((rows, wz), F32),
             pltpu.VMEM((nz, rows, wz), BF16),
             pltpu.VMEM((ne, CAP, LANE), F32),
             pltpu.VMEM((ne, CAP, LANE), F32),
             pltpu.VMEM((nf, 8, rows), F32),
             pltpu.VMEM((width, ff), BF16),
             pltpu.VMEM((ff, width), BF16),
+            pltpu.VMEM((ne, CAP, nz * LANE), BF16),
+            pltpu.VMEM((ne, CAP, nz * LANE), BF16),
+            pltpu.VMEM((nz, rows, LANE), BF16),
+            pltpu.VMEM((nz, rows, LANE), BF16),
             dma((2,)),
             dma((ne,)), dma((ne,)), dma((ne,)), dma((ne,)),
             ring_sems, ring_sems, ring_sems, ring_sems,
@@ -462,7 +554,8 @@
             ring_sems, ring_sems,
             dma((ne,)), dma((ne,)),
             dma((nf,)), dma((nf,)),
-            dma((6,)),
+            dma((ne,)), dma((ne,)), dma((nz,)), dma((nz,)),
+            dma((7,)),
         ],
         compiler_params=pltpu.CompilerParams(
             collective_id=0, has_side_effects=True, vmem_limit_bytes=62 * 1024 * 1024
@@ -471,6 +564,14 @@
         tokens, cotangent, expert_ids.T, gate_values.T,
         w_in.reshape(width, ff), w_out.reshape(ff, width),
     )
+    out = pl.pallas_call(
+        passing,
+        out_shape=tuple(jax.ShapeDtypeStruct(a.shape, a.dtype) for a in out),
+        in_specs=[hbm] * 4,
+        out_specs=(hbm,) * 4,
+        scratch_shapes=[pltpu.VMEM(a.shape, a.dtype) for a in out] + [dma((2, 4, PIECES))],
+        compiler_params=pltpu.CompilerParams(vmem_limit_bytes=62 * 1024 * 1024),
+    )(*out)
     return (
         out[0],
         out[1].T,

time: 150 us -> 146 us (0.973)
  local copies, waits for them, and re-layouts: 8.12 us -> 0 us
  Pallas kernels: 140 us -> 145 us
    unnamed x6 -> x0, local copies, waits for them, and re-layouts: 8.12 us -> none
    pallas_call x0 -> x1, Pallas kernels: none -> 4.9 us  [local(): pl.pallas_call(passing, out_shape=tuple((jax.ShapeDtypeStruct(a.shape, a....]
where the time goes in v4:
time: 146 us
  Pallas kernels  145 us (99%)
    pallas_call x1, Pallas kernels, local(): pl.pallas_call(functools.partial(kernel, nf, ne), out_shape=(jax.ShapeDty...  140 us
    pallas_call x1, Pallas kernels, local(): pl.pallas_call(passing, out_shape=tuple((jax.ShapeDtypeStruct(a.shape, a....  4.9 us

profile of v4, /device:TPU:6, one launch (start us, length us, event | category | flops | bytes accessed | tf_op | source)
XLA Modules:
  0.0 145.9 jit_solution(5535574638082326080)
XLA Ops:
  0.6 140.3 %shard_map.93 = (bf16[128,3072]{1,0:T(8,128)(2,1)}, bf16[4,128]{1,0:T(4,128)(2,1)}, bf16[3072,384]{1,0:T(8,128)(2,1)}, bf16[384,3072]{1,0:T(8,128)(2,1)}) custom-call(bf16[128,3072]{1,0:T(8,128)(2,1)} %tok_ref.1, bf16[128,3072]{1,0:T(8,128)(2,1)} %cot_ref.1, s32[4,128]{1,0:T(4,128)} %bitcast.9, bf16[4,128]{1,0:T(4,128)(2,1)} %bitcast.10, ...), custom_call_target="tpu_custom_call" | custom-call | tf_op jit(solution)/shard_map/pallas_call | solution.py:509
  141.0 4.9 %shard_map.94 = (bf16[128,3072]{1,0:T(8,128)(2,1)}, bf16[4,128]{1,0:T(4,128)(2,1)}, bf16[3072,384]{1,0:T(8,128)(2,1)}, bf16[384,3072]{1,0:T(8,128)(2,1)}) custom-call(bf16[128,3072]{1,0:T(8,128)(2,1)} %get-tuple-element.12.a0, bf16[4,128]{1,0:T(4,128)(2,1)} %get-tuple-element.13.a1, bf16[3072,384]{1,0:T(8,128)(2,1)} %get-tuple-element.14.a2, ...), custom_call_target="tpu_custom_call" | custom-call | tf_op jit(solution)/shard_map/pallas_call | solution.py:567

commit v5 on v4

--- a/solution.py
+++ b/solution.py
@@ -372,9 +372,8 @@
             lax.fori_loop(1, ne, d_start, 0)
             own_d.start()
         grads(i * nz // far, (i + 1) * nz // far)
-        if i == 0:
+        if i == far - 1:
             gates_pass()
-        if i == max(far - 2, 0):
             direct_combine()
     store_in = pltpu.make_async_copy(gin, gin_hbm, st_sem.at[3])
     store_out = pltpu.make_async_copy(gout, gout_hbm, st_sem.at[4])

time: 146 us -> 135 us (0.925)
  Pallas kernels: 145 us -> 133 us
    pallas_call x1, Pallas kernels: 140 us -> 128 us  [local(): pl.pallas_call(functools.partial(kernel, nf, ne), out_shape=(jax.ShapeDty...]
where the time goes in v5:
time: 135 us; the launch traced here: 133 us
  Pallas kernels  133 us (99%)
    pallas_call x1, Pallas kernels, local(): pl.pallas_call(functools.partial(kernel, nf, ne), out_shape=(jax.ShapeDty...  128 us
    pallas_call x1, Pallas kernels, local(): pl.pallas_call(passing, out_shape=tuple((jax.ShapeDtypeStruct(a.shape, a....  4.9 us

profile of v5, /device:TPU:6, one launch (start us, length us, event | category | flops | bytes accessed | tf_op | source)
XLA Modules:
  0.0 133.5 jit_solution(16819775843076447924)
XLA Ops:
  0.6 127.9 %shard_map.93 = (bf16[128,3072]{1,0:T(8,128)(2,1)}, bf16[4,128]{1,0:T(4,128)(2,1)}, bf16[3072,384]{1,0:T(8,128)(2,1)}, bf16[384,3072]{1,0:T(8,128)(2,1)}) custom-call(bf16[128,3072]{1,0:T(8,128)(2,1)} %tok_ref.1, bf16[128,3072]{1,0:T(8,128)(2,1)} %cot_ref.1, s32[4,128]{1,0:T(4,128)} %bitcast.9, bf16[4,128]{1,0:T(4,128)(2,1)} %bitcast.10, ...), custom_call_target="tpu_custom_call" | custom-call | tf_op jit(solution)/shard_map/pallas_call | solution.py:508
  128.6 4.9 %shard_map.94 = (bf16[128,3072]{1,0:T(8,128)(2,1)}, bf16[4,128]{1,0:T(4,128)(2,1)}, bf16[3072,384]{1,0:T(8,128)(2,1)}, bf16[384,3072]{1,0:T(8,128)(2,1)}) custom-call(bf16[128,3072]{1,0:T(8,128)(2,1)} %get-tuple-element.12.a0, bf16[4,128]{1,0:T(4,128)(2,1)} %get-tuple-element.13.a1, bf16[3072,384]{1,0:T(8,128)(2,1)} %get-tuple-element.14.a2, ...), custom_call_target="tpu_custom_call" | custom-call | tf_op jit(solution)/shard_map/pallas_call | solution.py:566

commit v6 on v5

--- a/solution.py
+++ b/solution.py
@@ -38,7 +38,7 @@
     rs_send, rs_recv, back_send, back_recv, pair_send, pair_recv, tok_all,
     gs_send, gs_recv, gf_all, gin, gout, d_send, d_recv, ts_send, ts_recv,
     load_sem, x_ss, x_rs, g_ss, g_rs, xr_ss, xr_rs, rs_ss, rs_rs, bk_ss, bk_rs,
-    pr_ss, pr_rs, tr_ss, tr_rs, gs_ss, gs_rs, gf_ss, gf_rs, d_ss, d_rs, ts_ss, ts_rs, st_sem,
+    pr_ss, pr_rs, tr_ss, tr_rs, gs_ss, gs_rs, gf_ss, gf_rs, d_ss, d_rs, ts_ss, ts_rs, sw_ss, sw_rs, st_sem,
 ):
     me_f, me_e = lax.axis_index("fsdp"), lax.axis_index("expert")
     nz = nf // 2
@@ -52,6 +52,8 @@
     sub = LANE
     wr = wz - sub
     pair_f = (1 - lo) * nz + z
+    wg = nz * LANE
+    wd = width - wg
     right_f = lo * nz + (z + 1) % nz
     left_f = lo * nz + (z + nz - 1) % nz
 
@@ -64,10 +66,22 @@
             device_id=dev(f, e), device_id_type=MESH,
         )
 
+    def near(e):
+        return (lo + (e // 2) % 2 + (me_e // 2) % 2) % 2
+
+    def near_f(e):
+        return near(e) * nz + z
+
     barrier = pltpu.get_barrier_semaphore()
 
     def greet_e(k, c):
-        pl.semaphore_signal(barrier, inc=1, device_id=dev(me_f, (me_e + k) % ne), device_id_type=MESH)
+        e = (me_e + k) % ne
+        pl.semaphore_signal(barrier, inc=1, device_id=dev(me_f, e), device_id_type=MESH)
+
+        @pl.when(near(e) != lo)
+        def _():
+            pl.semaphore_signal(barrier, inc=1, device_id=dev(near_f(e), e), device_id_type=MESH)
+
         return c
 
     def greet_f(k, c):
@@ -102,40 +116,54 @@
         one = jnp.where(slot_no == place[e : e + 1, :], 1.0, 0.0)
         sel32[e] = one
         gate_col = jnp.sum(one * gate_of[e : e + 1, :], axis=1, keepdims=True)
-        send_g[e, :, width:] = jnp.broadcast_to(gate_col, (CAP, LANE)).astype(BF16)
+        send_g[e, :, wd:] = jnp.broadcast_to(gate_col, (CAP, LANE)).astype(BF16)
     sel[...] = sel32[...].reshape(slots, rows).astype(BF16)
     pick = sel[...]
     cols = pl.ds(pl.multiple_of(z * wz, LANE), wz)
-    send_x[...] = blocks(jnp.dot(pick, tok_ref[:, cols], preferred_element_type=F32)).astype(BF16)
-
-    pl.semaphore_wait(barrier, (ne - 1) + (nf - 1))
+    send_x[:, :, :wz] = blocks(
+        jnp.dot(pick, tok_ref[:, cols], preferred_element_type=F32)
+    ).astype(BF16)
+    gcol = pl.ds(pl.multiple_of(z * LANE, LANE), LANE)
+    send_x[:, :, wz:] = blocks(
+        jnp.dot(pick, cot_ref[:, gcol], preferred_element_type=F32)
+    ).astype(BF16)
+
+    pl.semaphore_wait(barrier, (ne - 1) + (nf - 1) + ne // 2)
+
+    def side(l):
+        return pl.ds(pl.multiple_of(l * LANE, LANE), wz)
 
     def x_copy(k):
         e = (me_e + k) % ne
-        return remote(send_x.at[e], x_all.at[z, me_e], x_ss.at[e], x_rs.at[me_e], me_f, e)
+        c = side(near(e))
+        return remote(
+            send_x.at[e, :, c], x_all.at[z, me_e, :, c], x_ss.at[e], x_rs.at[me_e], near_f(e), e
+        )
 
     def x_start(k, c):
         x_copy(k).start()
         return c
 
     lax.fori_loop(1, ne, x_start, 0)
-    own_x = pltpu.make_async_copy(send_x.at[me_e], x_all.at[z, me_e], st_sem.at[0])
+    own_x = pltpu.make_async_copy(
+        send_x.at[me_e, :, side(lo)], x_all.at[z, me_e, :, side(lo)], st_sem.at[0]
+    )
     own_x.start()
 
-    gw = width // 6 if width % (6 * LANE) == 0 else width
+    gw = 4 * LANE
 
     def g_build(j, c):
-        span = pl.ds(pl.multiple_of(j * gw, LANE), gw)
-        send_g[:, :, span] = blocks(
-            jnp.dot(sel[...], cot_ref[:, span], preferred_element_type=F32)
+        src = pl.ds(pl.multiple_of(wg + j * gw, LANE), gw)
+        send_g[:, :, pl.ds(pl.multiple_of(j * gw, LANE), gw)] = blocks(
+            jnp.dot(sel[...], cot_ref[:, src], preferred_element_type=F32)
         ).astype(BF16)
         return c
 
-    lax.fori_loop(0, width // gw, g_build, 0)
+    lax.fori_loop(0, wd // gw, g_build, 0)
 
     def g_start(k, c):
         e = (me_e + k) % ne
-        remote(send_g.at[e], g_all.at[me_e], g_ss.at[e], g_rs.at[me_e], me_f, e).start()
+        remote(send_g.at[e], g_all.at[me_e], g_ss.at[e], g_rs.at[me_e], near_f(e), e).start()
         return c
 
     lax.fori_loop(1, ne, g_start, 0)
@@ -144,7 +172,10 @@
 
     def x_wait(k, c):
         b = (me_e + ne - k) % ne
-        remote(send_x.at[b], x_all.at[z, b], x_ss.at[b], x_rs.at[b], me_f, b).wait_recv()
+        c2 = side(lo)
+        remote(
+            send_x.at[b, :, c2], x_all.at[z, b, :, c2], x_ss.at[b], x_rs.at[b], near_f(b), b
+        ).wait_recv()
         return c
 
     lax.fori_loop(1, ne, x_wait, 0)
@@ -171,7 +202,7 @@
             right_f if direction == 0 else left_f, me_e,
         )
 
-    def ring(buf, lead, ss, rs, between):
+    def ring(buf, lead, ss, rs, between, arrived=None):
         for i in range(far + 1):
             for h in (0, 1):
                 for d in (0, 1):
@@ -179,6 +210,8 @@
                         ring_arrival(buf, lead, ss, rs, d, h, i - 1).wait_recv()
                     if i < hops(d, h):
                         ring_copy(buf, lead, ss, rs, d, h, i).start()
+                    if arrived is not None and 0 < i <= hops(d, h):
+                        arrived((z + nz - i) % nz if d == 0 else (z + i) % nz, h)
             between(i)
 
     def ring_drain(buf, lead, ss, rs):
@@ -189,13 +222,21 @@
                         ring_copy(buf, lead, ss, rs, d, h, i).wait_send()
 
     def x_lead(buf, piece, h):
-        return buf.at[piece, pl.ds(h * he, he)]
+        return buf.at[piece, pl.ds(h * he, he), :, side(lo)]
+
+    def swap(c, h, l):
+        ref = x_all.at[c, pl.ds(h * he, he), :, pl.ds(pl.multiple_of(l * wz, LANE), LANE)]
+        return remote(ref, ref, sw_ss.at[c, h], sw_rs.at[c, h], pair_f, me_e)
 
     def add_pre(c):
         w_rows = win[pl.ds(pl.multiple_of(c * wz, LANE), wz), :]
         for h in (0, 1):
-            xs = flat(x_all[c, h * he : (h + 1) * he])
+            swap(c, h, 1 - lo).wait_recv()
+            xs = flat(x_all[c, h * he : (h + 1) * he, :, :wz])
             x2[c, h * hs : (h + 1) * hs, :] = xs
+            g2[h * hs : (h + 1) * hs, pl.ds(pl.multiple_of(c * LANE, LANE), LANE)] = flat(
+                x_all[c, h * he : (h + 1) * he, :, wz:]
+            )
             pre[h * hs : (h + 1) * hs, :] += jnp.dot(xs, w_rows, preferred_element_type=F32)
 
     pre[...] = jnp.zeros_like(pre)
@@ -203,20 +244,23 @@
     def x_between(i):
         if i == 0:
             load_in.wait()
+        elif i == 1:
             add_pre(z)
-            return
-        add_pre((z + nz - i) % nz)
-        if i < far:
-            add_pre((z + i) % nz)
-
-    ring(x_all, x_lead, xr_ss, xr_rs, x_between)
+        else:
+            add_pre((z + nz - i + 1) % nz)
+            add_pre((z + i - 1) % nz)
+
+    swap(z, 0, lo).start()
+    swap(z, 1, lo).start()
+    ring(x_all, x_lead, xr_ss, xr_rs, x_between, lambda c, h: swap(c, h, lo).start())
+    add_pre((z + far) % nz)
 
     def g_arrival(b):
-        return remote(send_g.at[b], g_all.at[b], g_ss.at[b], g_rs.at[b], me_f, b)
+        return remote(send_g.at[b], g_all.at[b], g_ss.at[b], g_rs.at[b], near_f(b), b)
 
     def g_flat(p):
-        g2[pl.ds(pl.multiple_of(p * 2 * CAP, 16), 2 * CAP), :] = flat(
-            g_all[pl.ds(2 * p, 2), :, :width]
+        g2[pl.ds(pl.multiple_of(p * 2 * CAP, 16), 2 * CAP), wg:] = flat(
+            g_all[pl.ds(2 * p, 2), :, :wd]
         )
 
     own_g.wait()
@@ -236,7 +280,7 @@
     for h in (0, 1):
         span = slice(h * hs, (h + 1) * hs)
         up = nt(g2[span, :], wout[...])
-        gate = g_all[h * he : (h + 1) * he, :, width:].astype(F32).reshape(hs, LANE)
+        gate = g_all[h * he : (h + 1) * he, :, wd:].astype(F32).reshape(hs, LANE)
         gate = jnp.concatenate([gate] * (ff // LANE), axis=1)
         p = pre[span, :]
         squash = jax.nn.sigmoid(p)
@@ -438,8 +482,8 @@
 
     def drain(k, c):
         e = (me_e + k) % ne
-        remote(send_x.at[e], x_all.at[z, me_e], x_ss.at[e], x_rs.at[me_e], me_f, e).wait_send()
-        remote(send_g.at[e], g_all.at[me_e], g_ss.at[e], g_rs.at[me_e], me_f, e).wait_send()
+        x_copy(k).wait_send()
+        remote(send_g.at[e], g_all.at[me_e], g_ss.at[e], g_rs.at[me_e], near_f(e), e).wait_send()
         remote(gs_send.at[e], gs_recv.at[me_e], gs_ss.at[e], gs_rs.at[me_e], me_f, e).wait_send()
         remote(d_send.at[e], d_recv.at[me_e], d_ss.at[e], d_rs.at[me_e], me_f, e).wait_send()
         remote(back_send.at[e], back_recv.at[me_e], bk_ss.at[e], bk_rs.at[me_e], me_f, e).wait_send()
@@ -462,6 +506,13 @@
 
     lax.fori_loop(1, nz, drain_z, 0)
     ring_drain(x_all, x_lead, xr_ss, xr_rs)
+
+    def drain_swap(c, carry):
+        for h in (0, 1):
+            swap(c, h, lo).wait_send()
+        return carry
+
+    lax.fori_loop(0, nz, drain_swap, 0)
     ring_drain(tok_all, t_lead, tr_ss, tr_rs)
     for i in range(far):
         for h in (0, 1):
@@ -522,10 +573,10 @@
             pltpu.VMEM((ne * CAP, rows), BF16),
             pltpu.VMEM((nz, ne * CAP, wz), BF16),
             pltpu.VMEM((ne * CAP, width), BF16),
-            pltpu.VMEM((ne, CAP, wz), BF16),
-            pltpu.VMEM((nz, ne, CAP, wz), BF16),
-            pltpu.VMEM((ne, CAP, width + LANE), BF16),
-            pltpu.VMEM((ne, CAP, width + LANE), BF16),
+            pltpu.VMEM((ne, CAP, wz + LANE), BF16),
+            pltpu.VMEM((nz, ne, CAP, wz + LANE), BF16),
+            pltpu.VMEM((ne, CAP, width - nz * LANE + LANE), BF16),
+            pltpu.VMEM((ne, CAP, width - nz * LANE + LANE), BF16),
             pltpu.VMEM((ne * CAP, ff), F32),
             pltpu.VMEM((ne * CAP, ff), BF16),
             pltpu.VMEM((ne * CAP, ff), BF16),
@@ -554,6 +605,7 @@
             dma((ne,)), dma((ne,)),
             dma((nf,)), dma((nf,)),
             dma((ne,)), dma((ne,)), dma((nz,)), dma((nz,)),
+            dma((nz, 2)), dma((nz, 2)),
             dma((7,)),
         ],
         compiler_params=pltpu.CompilerParams(

time: 135 us -> 139 us (1.030)
  Pallas kernels: 133 us -> 136 us
    pallas_call x1, Pallas kernels: 128 us -> 131 us  [local(): pl.pallas_call(functools.partial(kernel, nf, ne), out_shape=(jax.ShapeDty...]
where the time goes in v6:
time: 139 us; the launch traced here: 137 us
  Pallas kernels  136 us (98%)
    pallas_call x1, Pallas kernels, local(): pl.pallas_call(functools.partial(kernel, nf, ne), out_shape=(jax.ShapeDty...  131 us
    pallas_call x1, Pallas kernels, local(): pl.pallas_call(passing, out_shape=tuple((jax.ShapeDtypeStruct(a.shape, a....  4.9 us

profile of v6, /device:TPU:6, one launch (start us, length us, event | category | flops | bytes accessed | tf_op | source)
XLA Modules:
  0.0 136.7 jit_solution(11992603795245037346)
XLA Ops:
  0.6 131.1 %shard_map.93 = (bf16[128,3072]{1,0:T(8,128)(2,1)}, bf16[4,128]{1,0:T(4,128)(2,1)}, bf16[3072,384]{1,0:T(8,128)(2,1)}, bf16[384,3072]{1,0:T(8,128)(2,1)}) custom-call(bf16[128,3072]{1,0:T(8,128)(2,1)} %tok_ref.1, bf16[128,3072]{1,0:T(8,128)(2,1)} %cot_ref.1, s32[4,128]{1,0:T(4,128)} %bitcast.9, bf16[4,128]{1,0:T(4,128)(2,1)} %bitcast.10, ...), custom_call_target="tpu_custom_call" | custom-call | tf_op jit(solution)/shard_map/pallas_call | solution.py:559
  131.8 4.9 %shard_map.94 = (bf16[128,3072]{1,0:T(8,128)(2,1)}, bf16[4,128]{1,0:T(4,128)(2,1)}, bf16[3072,384]{1,0:T(8,128)(2,1)}, bf16[384,3072]{1,0:T(8,128)(2,1)}) custom-call(bf16[128,3072]{1,0:T(8,128)(2,1)} %get-tuple-element.12.a0, bf16[4,128]{1,0:T(4,128)(2,1)} %get-tuple-element.13.a1, bf16[3072,384]{1,0:T(8,128)(2,1)} %get-tuple-element.14.a2, ...), custom_call_target="tpu_custom_call" | custom-call | tf_op jit(solution)/shard_map/pallas_call | solution.py:618

commit v7 on v5

--- a/solution.py
+++ b/solution.py
@@ -38,7 +38,7 @@
     rs_send, rs_recv, back_send, back_recv, pair_send, pair_recv, tok_all,
     gs_send, gs_recv, gf_all, gin, gout, d_send, d_recv, ts_send, ts_recv,
     load_sem, x_ss, x_rs, g_ss, g_rs, xr_ss, xr_rs, rs_ss, rs_rs, bk_ss, bk_rs,
-    pr_ss, pr_rs, tr_ss, tr_rs, gs_ss, gs_rs, gf_ss, gf_rs, d_ss, d_rs, ts_ss, ts_rs, st_sem,
+    pr_ss, pr_rs, tr_ss, tr_rs, gs_ss, gs_rs, gf_ss, gf_rs, d_ss, d_rs, ts_ss, ts_rs, sw_ss, sw_rs, st_sem,
 ):
     me_f, me_e = lax.axis_index("fsdp"), lax.axis_index("expert")
     nz = nf // 2
@@ -138,7 +138,6 @@
         remote(send_g.at[e], g_all.at[me_e], g_ss.at[e], g_rs.at[me_e], me_f, e).start()
         return c
 
-    lax.fori_loop(1, ne, g_start, 0)
     own_g = pltpu.make_async_copy(send_g.at[me_e], g_all.at[me_e], st_sem.at[1])
     own_g.start()
 
@@ -149,6 +148,7 @@
 
     lax.fori_loop(1, ne, x_wait, 0)
     own_x.wait()
+    lax.fori_loop(1, ne, g_start, 0)
 
     far = nz // 2
 
@@ -171,7 +171,7 @@
             right_f if direction == 0 else left_f, me_e,
         )
 
-    def ring(buf, lead, ss, rs, between):
+    def ring(buf, lead, ss, rs, between, arrived=None):
         for i in range(far + 1):
             for h in (0, 1):
                 for d in (0, 1):
@@ -179,6 +179,8 @@
                         ring_arrival(buf, lead, ss, rs, d, h, i - 1).wait_recv()
                     if i < hops(d, h):
                         ring_copy(buf, lead, ss, rs, d, h, i).start()
+                    if arrived is not None and 0 < i <= hops(d, h):
+                        arrived((z + nz - i) % nz if d == 0 else (z + i) % nz, h)
             between(i)
 
     def ring_drain(buf, lead, ss, rs):
@@ -422,17 +424,34 @@
     own_back.wait()
     tok = tn(sel[...], flat(back_recv[...]))
     pair_send[:, sub:] = tok
-    pair = remote(pair_send, pair_recv, pr_ss, pr_rs, pair_f, me_e)
+    hr = rows // 2
+    mine = pl.ds(pl.multiple_of(lo * hr, 16), hr)
+    other = pl.ds(pl.multiple_of((1 - lo) * hr, 16), hr)
+    pair = remote(pair_send.at[other], pair_recv.at[other], pr_ss, pr_rs, pair_f, me_e)
     pair.start()
-    pair.wait_recv()
-    tok_all[z] = (pair_send[...] + pair_recv[...]).astype(BF16)
-
-    hr = rows // 2
+    remote(pair_send.at[mine], pair_recv.at[mine], pr_ss, pr_rs, pair_f, me_e).wait_recv()
+    tok_all[z, mine, :] = (pair_send[mine, :] + pair_recv[mine, :]).astype(BF16)
+
+    def t_rows(piece, l, h):
+        return tok_all.at[piece, pl.ds(pl.multiple_of(l * hr + h * (hr // 2), 16), hr // 2)]
 
     def t_lead(buf, piece, h):
-        return buf.at[piece, pl.ds(h * hr, hr)]
-
-    ring(tok_all, t_lead, tr_ss, tr_rs, lambda i: None)
+        return t_rows(piece, lo, h)
+
+    def swap(c, h, l):
+        ref = t_rows(c, l, h)
+        return remote(ref, ref, sw_ss.at[c, h], sw_rs.at[c, h], pair_f, me_e)
+
+    def t_between(i):
+        if i == 0:
+            swap(z, 0, lo).start()
+            swap(z, 1, lo).start()
+
+    ring(tok_all, t_lead, tr_ss, tr_rs, t_between, lambda c, h: swap(c, h, lo).start())
+    for i in range(nz):
+        c = (z + (0, 1, nz - 1, 2, nz - 2, 3, nz - 3, 4)[i]) % nz if nz == 8 else i
+        for h in (0, 1):
+            swap(c, h, 1 - lo).wait_recv()
     for c in range(nz):
         out_ref[:, c * wz : (c + 1) * wz] = tok_all[c]
 
@@ -463,6 +482,13 @@
     lax.fori_loop(1, nz, drain_z, 0)
     ring_drain(x_all, x_lead, xr_ss, xr_rs)
     ring_drain(tok_all, t_lead, tr_ss, tr_rs)
+
+    def drain_swap(c, carry):
+        for h in (0, 1):
+            swap(c, h, lo).wait_send()
+        return carry
+
+    lax.fori_loop(0, nz, drain_swap, 0)
     for i in range(far):
         for h in (0, 1):
             for d in (0, 1):
@@ -554,6 +580,7 @@
             dma((ne,)), dma((ne,)),
             dma((nf,)), dma((nf,)),
             dma((ne,)), dma((ne,)), dma((nz,)), dma((nz,)),
+            dma((nz, 2)), dma((nz, 2)),
             dma((7,)),
         ],
         compiler_params=pltpu.CompilerParams(

time: 135 us -> 133 us (0.985)
  no operation moved by 1% of the time
where the time goes in v7:
time: 133 us
  Pallas kernels  132 us (99%)
    pallas_call x1, Pallas kernels, local(): pl.pallas_call(functools.partial(kernel, nf, ne), out_shape=(jax.ShapeDty...  127 us
    pallas_call x1, Pallas kernels, local(): pl.pallas_call(passing, out_shape=tuple((jax.ShapeDtypeStruct(a.shape, a....  4.9 us

profile of v7, /device:TPU:6, one launch (start us, length us, event | category | flops | bytes accessed | tf_op | source)
XLA Modules:
  0.0 132.8 jit_solution(2697300135167364484)
XLA Ops:
  0.6 127.2 %shard_map.93 = (bf16[128,3072]{1,0:T(8,128)(2,1)}, bf16[4,128]{1,0:T(4,128)(2,1)}, bf16[3072,384]{1,0:T(8,128)(2,1)}, bf16[384,3072]{1,0:T(8,128)(2,1)}) custom-call(bf16[128,3072]{1,0:T(8,128)(2,1)} %tok_ref.1, bf16[128,3072]{1,0:T(8,128)(2,1)} %cot_ref.1, s32[4,128]{1,0:T(4,128)} %bitcast.9, bf16[4,128]{1,0:T(4,128)(2,1)} %bitcast.10, ...), custom_call_target="tpu_custom_call" | custom-call | tf_op jit(solution)/shard_map/pallas_call | solution.py:534
  127.9 4.9 %shard_map.94 = (bf16[128,3072]{1,0:T(8,128)(2,1)}, bf16[4,128]{1,0:T(4,128)(2,1)}, bf16[3072,384]{1,0:T(8,128)(2,1)}, bf16[384,3072]{1,0:T(8,128)(2,1)}) custom-call(bf16[128,3072]{1,0:T(8,128)(2,1)} %get-tuple-element.12.a0, bf16[4,128]{1,0:T(4,128)(2,1)} %get-tuple-element.13.a1, bf16[3072,384]{1,0:T(8,128)(2,1)} %get-tuple-element.14.a2, ...), custom_call_target="tpu_custom_call" | custom-call | tf_op jit(solution)/shard_map/pallas_call | solution.py:593

commit v8 on v7

--- a/solution.py
+++ b/solution.py
@@ -374,9 +374,6 @@
             lax.fori_loop(1, ne, d_start, 0)
             own_d.start()
         grads(i * nz // far, (i + 1) * nz // far)
-        if i == far - 1:
-            gates_pass()
-            direct_combine()
     store_in = pltpu.make_async_copy(gin, gin_hbm, st_sem.at[3])
     store_out = pltpu.make_async_copy(gout, gout_hbm, st_sem.at[4])
     store_in.start()
@@ -402,6 +399,8 @@
     lax.fori_loop(1, ne, back_start, 0)
     own_back = pltpu.make_async_copy(back_send.at[me_e], back_recv.at[me_e], st_sem.at[5])
     own_back.start()
+    direct_combine()
+    gates_pass()
 
     def gf_wait(k, c):
         f = (me_f + nf - k) % nf

time: 133 us -> 136 us (1.023); the launches traced: 133 us -> 134 us
  no operation moved by 1% of the time
where the time goes in v8:
time: 136 us; the launch traced here: 134 us
  Pallas kernels  133 us (98%)
    pallas_call x1, Pallas kernels, local(): pl.pallas_call(functools.partial(kernel, nf, ne), out_shape=(jax.ShapeDty...  128 us
    pallas_call x1, Pallas kernels, local(): pl.pallas_call(passing, out_shape=tuple((jax.ShapeDtypeStruct(a.shape, a....  4.9 us

profile of v8, /device:TPU:6, one launch (start us, length us, event | category | flops | bytes accessed | tf_op | source)
XLA Modules:
  0.0 134.0 jit_solution(10422174868243469906)
XLA Ops:
  0.6 128.4 %shard_map.93 = (bf16[128,3072]{1,0:T(8,128)(2,1)}, bf16[4,128]{1,0:T(4,128)(2,1)}, bf16[3072,384]{1,0:T(8,128)(2,1)}, bf16[384,3072]{1,0:T(8,128)(2,1)}) custom-call(bf16[128,3072]{1,0:T(8,128)(2,1)} %tok_ref.1, bf16[128,3072]{1,0:T(8,128)(2,1)} %cot_ref.1, s32[4,128]{1,0:T(4,128)} %bitcast.9, bf16[4,128]{1,0:T(4,128)(2,1)} %bitcast.10, ...), custom_call_target="tpu_custom_call" | custom-call | tf_op jit(solution)/shard_map/pallas_call | solution.py:533
  129.1 4.9 %shard_map.94 = (bf16[128,3072]{1,0:T(8,128)(2,1)}, bf16[4,128]{1,0:T(4,128)(2,1)}, bf16[3072,384]{1,0:T(8,128)(2,1)}, bf16[384,3072]{1,0:T(8,128)(2,1)}) custom-call(bf16[128,3072]{1,0:T(8,128)(2,1)} %get-tuple-element.12.a0, bf16[4,128]{1,0:T(4,128)(2,1)} %get-tuple-element.13.a1, bf16[3072,384]{1,0:T(8,128)(2,1)} %get-tuple-element.14.a2, ...), custom_call_target="tpu_custom_call" | custom-call | tf_op jit(solution)/shard_map/pallas_call | solution.py:592
